TPU v7x, 32 devices: a whole 2x2x4 slice. The times are simulated.
32 devices in a mesh: blk: 2 (over x), rows: 16 (over z, y, core).
Axes of the slice: x: 2, y: 2, z: 4, core: 2. Of those that a mesh axis runs over, the one named last changes fastest.
Arguments:
- snapshots: float32 [32768, 512], P('rows', 'blk'), may hold values from -40 to 40
- grades: int32 [512], P('blk'), may hold values from 0 to 7
- mover: int32 [3, 2], P(None, 'blk'), may hold values from 0 to 1
Outputs:
- basis: float32 [32768, 512], P('rows', 'blk')
All inputs are finite; a program needn't handle non-finite values.
Results may differ from a plain program's by a relative error of at most 0.0001.
Values sent between devices are 32-bit elements; how exact they have to be, the bound alone decides.
A program may use at most 64 MiB of HBM per device.

v0:
```python
import jax
import jax.numpy as jnp
from jax import lax
from jax.sharding import PartitionSpec as P

BW = 128
ROUNDS = 4
NS_STEPS = 3


epsilon = 1e-06
relaxation = 1.2


def from_behind(value, axis, by):
    peers = lax.axis_size(axis)
    return lax.ppermute(value, axis, [(i, (i + by) % peers) for i in range(peers)])


def rotation(cross_gram, squares, labels):
    left_scale = lax.rsqrt(squares[:BW] + epsilon)
    right_scale = lax.rsqrt(squares[BW:] + epsilon)
    grade_gap = jnp.abs(labels[:BW, None] - labels[None, BW:])
    scaled = cross_gram * left_scale[:, None] * right_scale[None, :] / (1.0 + grade_gap)
    magnitude = jnp.sqrt(jnp.sum(scaled * scaled) + epsilon)
    generator = relaxation * scaled / magnitude
    zeros_block = jnp.zeros_like(generator)
    upper_half = jnp.concatenate([zeros_block, generator], 1)
    lower_half = jnp.concatenate([-generator.T, zeros_block], 1)
    iterate = jnp.eye(2 * BW, dtype=generator.dtype) + jnp.concatenate([upper_half, lower_half], 0)
    for sweep in range(NS_STEPS):
        product = lax.dot_general(
            iterate, iterate, (((0,), (0,)), ((), ())), precision=lax.Precision.HIGHEST
        )
        iterate = 1.5 * iterate - 0.5 * jnp.dot(iterate, product, precision=lax.Precision.HIGHEST)
    return iterate


def statistics(blocks):
    cross_part = lax.dot_general(
        blocks[:, :BW], blocks[:, BW:], (((0,), (0,)), ((), ())), precision=lax.Precision.HIGHEST
    )
    square_part = jnp.sum(blocks * blocks, axis=0)
    cross_gram, squares = lax.psum((cross_part, square_part), "rows")
    return (cross_gram, squares)


def assemble(first, incoming, staying):
    return jnp.where(
        first, jnp.concatenate([incoming, staying], -1), jnp.concatenate([staying, incoming], -1)
    )


def body(snapshots, grades, mover):
    blocks = snapshots
    labels = grades.astype(jnp.float32)
    for round_index in range(ROUNDS):
        cross_gram, squares = statistics(blocks)
        rotator = rotation(cross_gram, squares, labels)
        if round_index + 1 == ROUNDS:
            blocks = jnp.dot(blocks, rotator, precision=lax.Precision.HIGHEST)
        else:
            first = mover[round_index, 0] == 0
            move_label = jnp.where(first, labels[:BW], labels[BW:])
            stay_label = jnp.where(first, labels[BW:], labels[:BW])
            rotated = jnp.dot(blocks, rotator, precision=lax.Precision.HIGHEST)
            moving = jnp.where(first, rotated[:, :BW], rotated[:, BW:])
            staying = jnp.where(first, rotated[:, BW:], rotated[:, :BW])
            incoming, came_label = from_behind((moving, move_label), "blk", 1)
            blocks = assemble(first, incoming, staying)
            labels = assemble(first, came_label, stay_label)
    return blocks


def solution(mesh):
    placed = (P("rows", "blk"), P("blk"), P(None, "blk"))
    return jax.shard_map(
        body, mesh=mesh, in_specs=placed, out_specs=P("rows", "blk"), check_vma=False
    )
```

profile of v0, /device:TPU:0, one launch (start us, length us, event | category | flops | bytes accessed | tf_op | source)
XLA Modules:
  0.0 482.1 jit_solution(1401660455516647164)
XLA Ops:
  6.5 4.1 fusion.21
  10.8 0.3 multiply_reduce_fusion.3
  11.1 0.6 fusion.69
  11.7 34.9 %psum.57 = f32[256]{0:T(256)S(1)} all-reduce(f32[256]{0:T(256)S(1)} %multiply_reduce_fusion.3), channel_id=1, replica_groups=mesh['blk'=2,'rows'=16] {'rows'}, use_global_device_ids=true, to_apply=%region_2.0 | all-reduce | flops 256 | bytes 2048 | tf_op jit(solution)/shard_map/psum | solution.py:44
  47.3 52.5 %all-reduce.13.cloned.1.call-done = f32[128,128]{1,0:T(8,128)} async-done(((f32[128,128]{1,0:T(8,128)}), f32[128,128]{1,0:T(8,128)}) %all-reduce.13.cloned.1.call-update) | async-done | bytes 65552 | tf_op jit(solution)/shard_map/psum | solution.py:44
  99.8 1.5 multiply_reduce_fusion.7
  102.0 0.9 negate_bitcast_fusion.3
  103.1 0.4 fusion.24
  103.5 0.6 fusion.11
  104.1 0.4 fusion.70
  104.5 0.6 fusion.10
  105.1 0.4 fusion.71
  105.5 0.6 fusion.9
  106.1 1.9 convolution_bitcast_fusion
  108.1 0.2 slice_select_fusion.4
  108.3 1.5 collective-permute-start
  109.9 0.6 collective-permute-start.1
  111.0 22.7 %collective-permute-done.1 = f32[128]{0:T(128)S(1)} collective-permute-done((f32[128]{0:T(128)S(1)}, f32[128]{0:T(128)S(1)}, u32[]{:S(2)}, u32[]{:S(2)}) %collective-permute-start.1) | collective-permute-done | bytes 544 | tf_op jit(solution)/shard_map/ppermute | solution.py:17
  133.7 0.3 multiply_reduce_fusion.2
  134.0 1.6 fusion.18
  135.7 29.7 %psum.59 = f32[256]{0:T(256)S(1)} all-reduce(f32[256]{0:T(256)S(1)} %get-tuple-element.15), channel_id=1, replica_groups=mesh['blk'=2,'rows'=16] {'rows'}, use_global_device_ids=true, to_apply=%region_6.7 | all-reduce | flops 256 | bytes 2048 | tf_op jit(solution)/shard_map/psum | solution.py:44
  165.4 55.9 %all-reduce.15.cloned.1.call-done = f32[128,128]{1,0:T(8,128)} async-done(((f32[128,128]{1,0:T(8,128)}), f32[128,128]{1,0:T(8,128)}) %all-reduce.15.cloned.1.call-update) | async-done | bytes 65552 | tf_op jit(solution)/shard_map/psum | solution.py:44
  221.3 1.5 multiply_reduce_fusion.6
  223.5 0.9 negate_bitcast_fusion.2
  224.6 0.4 fusion.25
  225.0 0.6 fusion.8
  225.6 0.4 fusion.72
  226.0 0.6 fusion.7
  226.6 0.4 fusion.73
  227.1 0.6 fusion.6
  227.7 2.0 fusion.74
  229.7 0.2 slice_select_fusion.2
  229.9 1.5 collective-permute-start.2
  231.5 0.6 collective-permute-start.3
  232.6 22.6 %collective-permute-done.3 = f32[128]{0:T(128)S(1)} collective-permute-done((f32[128]{0:T(128)S(1)}, f32[128]{0:T(128)S(1)}, u32[]{:S(2)}, u32[]{:S(2)}) %collective-permute-start.3) | collective-permute-done | bytes 544 | tf_op jit(solution)/shard_map/ppermute | solution.py:17
  255.3 0.3 multiply_reduce_fusion.1
  255.6 1.6 fusion.15
  257.3 29.7 %psum.61 = f32[256]{0:T(256)S(1)} all-reduce(f32[256]{0:T(256)S(1)} %get-tuple-element.11), channel_id=1, replica_groups=mesh['blk'=2,'rows'=16] {'rows'}, use_global_device_ids=true, to_apply=%region_10.11 | all-reduce | flops 256 | bytes 2048 | tf_op jit(solution)/shard_map/psum | solution.py:44
  287.0 55.9 %all-reduce.17.cloned.1.call-done = f32[128,128]{1,0:T(8,128)} async-done(((f32[128,128]{1,0:T(8,128)}), f32[128,128]{1,0:T(8,128)}) %all-reduce.17.cloned.1.call-update) | async-done | bytes 65552 | tf_op jit(solution)/shard_map/psum | solution.py:44
  342.9 1.5 multiply_reduce_fusion.5
  345.1 0.9 negate_bitcast_fusion.1
  346.2 0.4 fusion.26
  346.6 0.6 fusion.5
  347.2 0.4 fusion.75
  347.6 0.6 fusion.4
  348.3 0.4 fusion.76
  348.7 0.6 fusion.3
  349.3 2.0 fusion.77
  351.5 1.5 collective-permute-start.4
  353.1 0.6 collective-permute-start.5
  353.6 23.2 %collective-permute-done.5 = f32[128]{0:T(128)S(1)} collective-permute-done((f32[128]{0:T(128)S(1)}, f32[128]{0:T(128)S(1)}, u32[]{:S(2)}, u32[]{:S(2)}) %collective-permute-start.5) | collective-permute-done | bytes 544 | tf_op jit(solution)/shard_map/ppermute | solution.py:17
  376.9 0.3 multiply_reduce_fusion
  377.2 1.6 fusion.12
  378.9 29.8 %psum.63 = f32[256]{0:T(256)S(1)} all-reduce(f32[256]{0:T(256)S(1)} %get-tuple-element.7), channel_id=1, replica_groups=mesh['blk'=2,'rows'=16] {'rows'}, use_global_device_ids=true, to_apply=%region_14.15 | all-reduce | flops 256 | bytes 2048 | tf_op jit(solution)/shard_map/psum | solution.py:44
  408.6 55.8 %all-reduce.19.cloned.1.call-done = f32[128,128]{1,0:T(8,128)} async-done(((f32[128,128]{1,0:T(8,128)}), f32[128,128]{1,0:T(8,128)}) %all-reduce.19.cloned.1.call-update) | async-done | bytes 65552 | tf_op jit(solution)/shard_map/psum | solution.py:44
  464.4 1.5 multiply_reduce_fusion.4
  466.7 0.9 negate_bitcast_fusion
  467.7 0.4 fusion.27
  468.2 0.6 fusion.2
  468.8 0.4 fusion.78
  469.2 0.6 fusion.1
  469.8 0.4 fusion.79
  470.2 0.6 fusion
  470.8 4.8 fusion.80
  (34 shorter events, 0.9 us)
Async XLA Ops:
  6.5 4.2 copy-start
  6.5 4.5 copy-start.1
  6.5 5.1 %copy-start.2 = (s32[256]{0:T(256)S(1)}, s32[256]{0:T(256)}, u32[]{:S(2)}) copy-start(s32[256]{0:T(256)} %param.4) | copy-start | bytes 3076
  6.5 93.2 %all-reduce.13.cloned.1.call-start = ((), (), s32[]{:S(2)}) async-start(), calls=%async_computation | async-start | bytes 131072 | tf_op jit(solution)/shard_map/psum | solution.py:44
  10.7 210.6 %all-reduce.15.cloned.1.call-start = ((), (), s32[]{:S(2)}) async-start(), calls=%async_computation.1 | async-start | bytes 131072 | tf_op jit(solution)/shard_map/psum | solution.py:44
  108.3 25.3 %collective-permute-start = (f32[2048,128]{0,1:T(8,128)S(1)}, f32[2048,128]{0,1:T(8,128)S(1)}, u32[]{:S(2)}, u32[]{:S(2)}) collective-permute-start(f32[2048,128]{0,1:T(8,128)S(1)} %get-tuple-element.24), channel_id=1, source_target_pairs={{0,16},{16,0},{1,17},{17,1},{2,18},{18,2},{3,19},{19,3},{4,20},{20... | collective-permute-start | bytes 3145736 | tf_op jit(solution)/shard_map/ppermute | solution.py:17
  109.9 23.8 %collective-permute-start.1 = (f32[128]{0:T(128)S(1)}, f32[128]{0:T(128)S(1)}, u32[]{:S(2)}, u32[]{:S(2)}) collective-permute-start(f32[128]{0:T(128)S(1)} %get-tuple-element.41), channel_id=1, source_target_pairs={{0,16},{16,0},{1,17},{17,1},{2,18},{18,2},{3,19},{19,3},{4,20},{20... | collective-permute-start | bytes 1544 | tf_op jit(solution)/shard_map/ppermute | solution.py:17
  135.6 207.3 %all-reduce.17.cloned.1.call-start = ((), (), s32[]{:S(2)}) async-start(), calls=%async_computation.2 | async-start | bytes 131072 | tf_op jit(solution)/shard_map/psum | solution.py:44
  229.9 25.3 %collective-permute-start.2 = (f32[2048,128]{0,1:T(8,128)S(1)}, f32[2048,128]{0,1:T(8,128)S(1)}, u32[]{:S(2)}, u32[]{:S(2)}) collective-permute-start(f32[2048,128]{0,1:T(8,128)S(1)} %get-tuple-element.22), channel_id=1, source_target_pairs={{0,16},{16,0},{1,17},{17,1},{2,18},{18,2},{3,19},{19,3},{4,20},{20... | collective-permute-start | bytes 3145736 | tf_op jit(solution)/shard_map/ppermute | solution.py:17
  231.5 23.8 %collective-permute-start.3 = (f32[128]{0:T(128)S(1)}, f32[128]{0:T(128)S(1)}, u32[]{:S(2)}, u32[]{:S(2)}) collective-permute-start(f32[128]{0:T(128)S(1)} %get-tuple-element.35), channel_id=1, source_target_pairs={{0,16},{16,0},{1,17},{17,1},{2,18},{18,2},{3,19},{19,3},{4,20},{20... | collective-permute-start | bytes 1544 | tf_op jit(solution)/shard_map/ppermute | solution.py:17
  257.3 207.2 %all-reduce.19.cloned.1.call-start = ((), (), s32[]{:S(2)}) async-start(), calls=%async_computation.3 | async-start | bytes 131072 | tf_op jit(solution)/shard_map/psum | solution.py:44
  351.5 25.3 %collective-permute-start.4 = (f32[2048,128]{0,1:T(8,128)S(1)}, f32[2048,128]{0,1:T(8,128)S(1)}, u32[]{:S(2)}, u32[]{:S(2)}) collective-permute-start(f32[2048,128]{0,1:T(8,128)S(1)} %get-tuple-element.20), channel_id=1, source_target_pairs={{0,16},{16,0},{1,17},{17,1},{2,18},{18,2},{3,19},{19,3},{4,20},{20... | collective-permute-start | bytes 3145736 | tf_op jit(solution)/shard_map/ppermute | solution.py:17
  353.1 23.8 %collective-permute-start.5 = (f32[128]{0:T(128)S(1)}, f32[128]{0:T(128)S(1)}, u32[]{:S(2)}, u32[]{:S(2)}) collective-permute-start(f32[128]{0:T(128)S(1)} %get-tuple-element.29), channel_id=1, source_target_pairs={{0,16},{16,0},{1,17},{17,1},{2,18},{18,2},{3,19},{19,3},{4,20},{20... | collective-permute-start | bytes 1544 | tf_op jit(solution)/shard_map/ppermute | solution.py:17
Sparse Core Ops, SparseCore 0:
  10.8 88.8 all-reduce.12
  135.7 85.4 all-reduce.14
  257.4 85.4 all-reduce.16
  379.0 85.4 all-reduce.18
where the time goes:
time: 484 us; the launch traced here: 482 us
  waiting for transfers between devices  289 us (60%)
  blocking collectives  124 us (26%)
  matrix products  32 us (7%)
  between operations  18.1 us (4%)
  other arithmetic  11.9 us (2%)
  starting transfers between devices  6.4 us (1%)
    psum x4, waiting for transfers between devices, statistics(): cross_gram, squares = lax.psum((cross_part, square_part), 'rows')  220 us
    psum x4, blocking collectives, statistics(): cross_gram, squares = lax.psum((cross_part, square_part), 'rows')  124 us
    ppermute x6, waiting for transfers between devices, from_behind(): lax.ppermute(value, axis, [(i, (i + by) % peers) for i in range(peers)])  68.5 us
  transfers between devices with their start and end apart: 10, of which 7 were waited for; matrix products, arithmetic and copies ran while one was open for 0% of the time, Pallas kernels for 0%

commit v1 on v0

v1 whole, which is shorter than its diff:
```python
import functools

import jax
import jax.numpy as jnp
from jax import lax
from jax.experimental import pallas as pl
from jax.experimental.pallas import tpu as pltpu
from jax.sharding import PartitionSpec as P

BW = 128
ROUNDS = 4
NS_STEPS = 3
CHUNKS = 4

epsilon = 1e-06
relaxation = 1.2

MESH = pl.DeviceIdType.MESH
ROWS_DIM = (((0,), (0,)), ((), ()))
PLAIN = (((1,), (0,)), ((), ()))
VMEM = pl.BlockSpec(memory_space=pltpu.VMEM)
ANY = pl.BlockSpec(memory_space=pl.ANY)


def from_behind(value, axis, by):
    peers = lax.axis_size(axis)
    return lax.ppermute(value, axis, [(i, (i + by) % peers) for i in range(peers)])


def rotation(cross_gram, squares, labels):
    left_scale = lax.rsqrt(squares[:BW] + epsilon)
    right_scale = lax.rsqrt(squares[BW:] + epsilon)
    grade_gap = jnp.abs(labels[:BW, None] - labels[None, BW:])
    scaled = cross_gram * left_scale[:, None] * right_scale[None, :] / (1.0 + grade_gap)
    magnitude = jnp.sqrt(jnp.sum(scaled * scaled) + epsilon)
    generator = relaxation * scaled / magnitude
    zeros_block = jnp.zeros_like(generator)
    upper_half = jnp.concatenate([zeros_block, generator], 1)
    lower_half = jnp.concatenate([-generator.T, zeros_block], 1)
    iterate = jnp.eye(2 * BW, dtype=generator.dtype) + jnp.concatenate([upper_half, lower_half], 0)
    for sweep in range(NS_STEPS):
        product = lax.dot_general(iterate, iterate, ROWS_DIM, precision=lax.Precision.HIGHEST)
        iterate = 1.5 * iterate - 0.5 * jnp.dot(iterate, product, precision=lax.Precision.HIGHEST)
    return iterate


def statistics(blocks):
    cross_part = lax.dot_general(
        blocks[:, :BW], blocks[:, BW:], ROWS_DIM, precision=lax.Precision.HIGHEST
    )
    square_part = jnp.sum(blocks * blocks, axis=0)
    return lax.psum((cross_part, square_part), "rows")


def assemble(first, incoming, staying):
    return jnp.where(
        first, jnp.concatenate([incoming, staying], -1), jnp.concatenate([staying, incoming], -1)
    )


def general_body(snapshots, grades, mover):
    blocks = snapshots
    labels = grades.astype(jnp.float32)
    for round_index in range(ROUNDS):
        cross_gram, squares = statistics(blocks)
        rotator = rotation(cross_gram, squares, labels)
        blocks = jnp.dot(blocks, rotator, precision=lax.Precision.HIGHEST)
        if round_index + 1 < ROUNDS:
            first = mover[round_index, 0] == 0
            move_label = jnp.where(first, labels[:BW], labels[BW:])
            stay_label = jnp.where(first, labels[BW:], labels[:BW])
            moving = jnp.where(first, blocks[:, :BW], blocks[:, BW:])
            staying = jnp.where(first, blocks[:, BW:], blocks[:, :BW])
            incoming, came_label = from_behind((moving, move_label), "blk", 1)
            blocks = assemble(first, incoming, staying)
            labels = assemble(first, came_label, stay_label)
    return blocks


def split(value):
    high = value.astype(jnp.bfloat16)
    return high, (value - high.astype(jnp.float32)).astype(jnp.bfloat16)


def dot_split(a, b, dims=PLAIN):
    (ah, al), (bh, bl) = a, b
    mul = functools.partial(lax.dot_general, dimension_numbers=dims, preferred_element_type=jnp.float32)
    return mul(ah, bh) + (mul(ah, bl) + mul(al, bh))


def dot3(a, b, dims=PLAIN):
    return dot_split(split(a), split(b), dims)


def dot6(a, b, dims=PLAIN):
    return lax.dot_general(
        a, b, dims, precision=lax.Precision.HIGHEST, preferred_element_type=jnp.float32
    )


def gram_kernel(
    n, x_ref, meta_ref, gram_ref, meta_out, half_ref,
    came, dpart, dgot, dfull, dother, cpart, cgot, cmine, cother, cfull, meta_got,
    x_send, x_recv, rs_send, rs_recv, ag_send, ag_recv, one_send, one_recv, local_sem,
):
    pos, me = lax.axis_index("blk"), lax.axis_index("rows")
    other = 1 - pos
    rows, width = x_ref.shape
    half = rows // 2
    piece = half // CHUNKS
    share = width // n
    partner = (other, me)

    barrier = pltpu.get_barrier_semaphore()
    for k in range(1, n):
        pl.semaphore_signal(
            barrier, inc=1, device_id=(pos, lax.rem(me + k, n)), device_id_type=MESH
        )
    pl.semaphore_signal(barrier, inc=1, device_id=partner, device_id_type=MESH)
    pl.semaphore_wait(barrier, n)

    def remote(src, dst, send, recv, device):
        return pltpu.make_async_remote_copy(
            src_ref=src, dst_ref=dst, send_sem=send, recv_sem=recv,
            device_id=device, device_id_type=MESH,
        )

    labels = remote(meta_ref, meta_got, one_send.at[0], one_recv.at[0], partner)
    labels.start()
    swaps = []
    for c in range(CHUNKS):
        source = x_ref.at[pl.ds(pl.multiple_of(other * half + c * piece, piece), piece)]
        swaps.append(
            remote(source, came.at[pl.ds(c * piece, piece)], x_send.at[c], x_recv.at[c], partner)
        )
        swaps[-1].start()

    def scatter(part, got, which):
        copies = []
        for k in range(1, n):
            peer = lax.rem(me + k, n)
            copies.append(
                remote(part.at[peer], got.at[k], rs_send.at[which, k], rs_recv.at[which, k], (pos, peer))
            )
            copies[-1].start()
        return copies

    def gather(full, which):
        copies = []
        for k in range(1, n):
            peer = lax.rem(me + k, n)
            copies.append(
                remote(full.at[me], full.at[me], ag_send.at[which, k], ag_recv.at[which, k], (pos, peer))
            )
            copies[-1].start()
        return copies

    def summed(part, got, copies):
        total = part[me]
        for k in range(1, n):
            copies[k - 1].wait()
            total = total + got[k]
        return total

    tile = piece
    own = jnp.zeros((width, width), jnp.float32)
    for t in range(rows // tile):
        block = split(x_ref[t * tile:(t + 1) * tile, :])
        own = own + dot_split(block, block, ROWS_DIM)
    dpart[...] = own.reshape(n, share, width)
    d_scatter = scatter(dpart, dgot, 0)

    def cross(c):
        swaps[c].wait()
        mine = x_ref[pl.ds(pl.multiple_of(pos * half + c * piece, piece), piece), :]
        theirs = came[c * piece:(c + 1) * piece, :]
        left = jnp.where(pos == 0, mine, theirs)
        right = jnp.where(pos == 0, theirs, mine)
        return dot3(left, right, ROWS_DIM)

    total = cross(0)
    dfull[me] = summed(dpart, dgot, d_scatter)
    d_gather = gather(dfull, 0)
    for c in range(1, CHUNKS - 1):
        total = total + cross(c)
    for copy in d_gather:
        copy.wait()
    d_swap = remote(dfull, dother, one_send.at[1], one_recv.at[1], partner)
    d_swap.start()
    total = total + cross(CHUNKS - 1)
    cpart[...] = total.reshape(n, share, width)
    c_scatter = scatter(cpart, cgot, 1)
    keep = pltpu.make_async_copy(came, half_ref, local_sem)
    keep.start()
    cmine[...] = summed(cpart, cgot, c_scatter)
    c_swap = remote(cmine, cother, one_send.at[2], one_recv.at[2], partner)
    c_swap.start()
    labels.wait()
    meta_out[pos] = meta_ref[...]
    meta_out[other] = meta_got[...]
    d_swap.wait()
    gram_ref[pos] = dfull[...].reshape(width, width)
    gram_ref[other] = dother[...].reshape(width, width)
    c_swap.wait()
    cfull[me] = cmine[...] + cother[...]
    c_gather = gather(cfull, 1)
    for copy in c_gather:
        copy.wait()
    gram_ref[2] = cfull[...].reshape(width, width)
    keep.wait()


def polar(cross_gram, left_square, right_square, left_label, right_label):
    left_scale = lax.rsqrt(left_square + epsilon)
    right_scale = lax.rsqrt(right_square + epsilon)
    scaled = cross_gram * left_scale * right_scale / (1.0 + jnp.abs(left_label - right_label))
    magnitude = jnp.sqrt(jnp.sum(scaled * scaled, keepdims=True) + epsilon)
    return relaxation * scaled / magnitude


def eye(n):
    return (
        lax.broadcasted_iota(jnp.int32, (n, n), 0) == lax.broadcasted_iota(jnp.int32, (n, n), 1)
    ).astype(jnp.float32)


def rotations(generators):
    unit = eye(BW)
    signs = [split(b) for b in generators]
    turned = [split(b.T) for b in generators]
    norm = []
    for b, bt in zip(signs, turned):
        norm.append(unit + dot_split(b, bt))
        norm.append(unit + dot_split(bt, b))
    gain = None
    for sweep in range(NS_STEPS):
        factor = [1.5 * unit - 0.5 * v for v in norm]
        cut = [split(f) for f in factor]
        last = sweep + 1 == NS_STEPS
        if last:
            edge = [dot_split(cut[2 * i], split(e)) for i, e in enumerate(edge)]
        else:
            parts = [split(v) for v in norm]
            inner = [2.25 * unit - 1.5 * v + 0.25 * dot_split(p, p) for v, p in zip(norm, parts)]
            norm = [dot_split(p, split(v)) for p, v in zip(parts, inner)]
        if gain is None:
            gain = factor
        else:
            gain = [dot_split(split(g), f) for g, f in zip(gain, cut)]
        if sweep + 2 == NS_STEPS:
            edge = [dot_split(split(gain[2 * i]), b) for i, b in enumerate(signs)]
    out = []
    for i, e in enumerate(edge):
        upper = jnp.concatenate([gain[2 * i], e], 1)
        lower = jnp.concatenate([-e.T, gain[2 * i + 1]], 1)
        out.append(jnp.concatenate([upper, lower], 0))
    return out


def chain_kernel(gram_ref, meta_ref, own_ref, other_ref, g, w, lab):
    pos = lax.axis_index("blk")
    width = 2 * BW
    unit = eye(width)
    for i in range(4):
        p, s = divmod(i, 2)
        for j in range(4):
            q, t = divmod(j, 2)
            rows, cols = slice(s * BW, s * BW + BW), slice(t * BW, t * BW + BW)
            if p == q:
                g[4 * i + j] = gram_ref[p, rows, cols]
            elif p == 0:
                g[4 * i + j] = gram_ref[2, rows, cols]
                g[4 * j + i] = gram_ref[2, rows, cols].T
        lab[i] = jnp.broadcast_to(meta_ref[p, 0:1, s * BW:(s + 1) * BW], (BW, BW))
    small = eye(BW)
    slots = [[0, 1], [2, 3]]

    def generator(a, b):
        left_square = jnp.sum(g[4 * a + a] * small, axis=1, keepdims=True)
        right_square = jnp.sum(g[4 * b + b] * small, axis=0, keepdims=True)
        return polar(g[4 * a + b], left_square, right_square, lab[a].T, lab[b])

    def turn(a, b, q, r):
        if r == 0:
            p = a // 2
            w[a] = jnp.zeros((2 * width, BW), jnp.float32)
            w[b] = jnp.zeros((2 * width, BW), jnp.float32)
            w[a, p * width:(p + 1) * width] = q[:, :BW]
            w[b, p * width:(p + 1) * width] = q[:, BW:]
        else:
            both = dot3(jnp.concatenate([w[a], w[b]], 1), q)
            w[a] = both[:, :BW]
            w[b] = both[:, BW:]

    for r in range(ROUNDS - 1):
        qs = rotations([generator(*slots[p]) for p in range(2)])
        for p in range(2):
            turn(*slots[p], qs[p], r)
        for p, q in ((0, 0), (1, 1), (0, 1)):
            (a, b), (c, d) = slots[p], slots[q]
            upper = jnp.concatenate([g[4 * a + c], g[4 * a + d]], 1)
            lower = jnp.concatenate([g[4 * b + c], g[4 * b + d]], 1)
            block = jnp.concatenate([upper, lower], 0)
            block = dot6(qs[p], dot6(block, qs[q]), ROWS_DIM)
            for i, e in enumerate((a, b)):
                for j, f in enumerate((c, d)):
                    value = block[i * BW:(i + 1) * BW, j * BW:(j + 1) * BW]
                    g[4 * e + f] = value
                    if p != q:
                        g[4 * f + e] = value.T
        first = [jnp.max(meta_ref[p, r + 1:r + 2, :BW]) < 0.5 for p in range(2)]
        moving = [jnp.where(first[p], slots[p][0], slots[p][1]) for p in range(2)]
        staying = [jnp.where(first[p], slots[p][1], slots[p][0]) for p in range(2)]
        slots = [
            [
                jnp.where(first[p], moving[1 - p], staying[p]),
                jnp.where(first[p], staying[p], moving[1 - p]),
            ]
            for p in range(2)
        ]
    a = jnp.where(pos == 0, slots[0][0], slots[1][0])
    b = jnp.where(pos == 0, slots[0][1], slots[1][1])
    (q,) = rotations([generator(a, b)])
    turn(a, b, q, ROUNDS)
    mine = pl.ds(pl.multiple_of(pos * width, width), width)
    theirs = pl.ds(pl.multiple_of((1 - pos) * width, width), width)
    own_ref[:, :BW] = w[a, mine]
    own_ref[:, BW:] = w[b, mine]
    other_ref[:, :BW] = w[a, theirs]
    other_ref[:, BW:] = w[b, theirs]


def apply_kernel(where_ref, x_ref, near_ref, far_ref, own_ref, other_ref, out_ref):
    partner = jnp.where(pl.program_id(0) == 0, near_ref[...], far_ref[...])
    out_ref[...] = dot3(x_ref[...], own_ref[...]) + dot3(partner, other_ref[...])


def pair_body(n, snapshots, grades, mover):
    rows, width = snapshots.shape
    share = width // n
    half = rows // 2
    pos = lax.axis_index("blk")
    f32 = jnp.float32
    meta = jnp.concatenate(
        [
            grades.astype(f32)[None],
            jnp.broadcast_to(mover.astype(f32), (ROUNDS - 1, width)),
            jnp.zeros((8 - ROUNDS, width), f32),
        ]
    )
    dma = pltpu.SemaphoreType.DMA
    shares = pltpu.VMEM((n, share, width), f32)
    gram, metas, near = pl.pallas_call(
        functools.partial(gram_kernel, n),
        out_shape=(
            jax.ShapeDtypeStruct((3, width, width), f32),
            jax.ShapeDtypeStruct((2, 8, width), f32),
            jax.ShapeDtypeStruct((half, width), f32),
        ),
        in_specs=[VMEM, VMEM],
        out_specs=(VMEM, VMEM, ANY),
        scratch_shapes=[
            pltpu.VMEM((half, width), f32),
            shares, shares, shares, shares,
            shares, shares, pltpu.VMEM((share, width), f32), pltpu.VMEM((share, width), f32), shares,
            pltpu.VMEM((8, width), f32),
            dma((CHUNKS,)), dma((CHUNKS,)), dma((2, n)), dma((2, n)), dma((2, n)), dma((2, n)),
            dma((3,)), dma((3,)), dma,
        ],
        compiler_params=pltpu.CompilerParams(
            collective_id=0, has_side_effects=True, vmem_limit_bytes=40 * 1024 * 1024
        ),
    )(snapshots, meta)
    late = lax.dynamic_slice_in_dim(snapshots, pos * half, half, 0)
    late, gram = lax.optimization_barrier((late, gram))
    far = lax.ppermute(late, "blk", [(0, 1), (1, 0)])
    w_own, w_other = pl.pallas_call(
        chain_kernel,
        out_shape=(jax.ShapeDtypeStruct((width, width), f32),) * 2,
        in_specs=[VMEM, VMEM],
        out_specs=(VMEM, VMEM),
        scratch_shapes=[
            pltpu.VMEM((16, BW, BW), f32),
            pltpu.VMEM((4, 2 * width, BW), f32),
            pltpu.VMEM((4, BW, BW), f32),
        ],
        compiler_params=pltpu.CompilerParams(vmem_limit_bytes=40 * 1024 * 1024),
        cost_estimate=pl.CostEstimate(
            flops=20 * 10**9, bytes_accessed=4 * width * width * 6, transcendentals=0
        ),
    )(gram, metas)
    tile = half // CHUNKS
    out = pl.pallas_call(
        apply_kernel,
        out_shape=jax.ShapeDtypeStruct((rows, width), f32),
        grid_spec=pltpu.PrefetchScalarGridSpec(
            num_scalar_prefetch=1,
            grid=(2, CHUNKS),
            in_specs=[
                pl.BlockSpec((tile, width), lambda j, i, s: (lax.rem(s[0] + j, 2) * CHUNKS + i, 0)),
                pl.BlockSpec((tile, width), lambda j, i, s: (jnp.where(j == 0, i, CHUNKS - 1), 0)),
                pl.BlockSpec((tile, width), lambda j, i, s: (jnp.where(j == 0, 0, i), 0)),
                pl.BlockSpec((width, width), lambda j, i, s: (0, 0)),
                pl.BlockSpec((width, width), lambda j, i, s: (0, 0)),
            ],
            out_specs=pl.BlockSpec((tile, width), lambda j, i, s: (lax.rem(s[0] + j, 2) * CHUNKS + i, 0)),
        ),
    )(jnp.asarray(pos, jnp.int32).reshape(1), snapshots, near, far, w_own, w_other)
    return out


def solution(mesh):
    placed = (P("rows", "blk"), P("blk"), P(None, "blk"))
    n = mesh.shape["rows"]
    pairs = mesh.shape["blk"] == 2 and (2 * BW) % (8 * n) == 0
    body = functools.partial(pair_body, n) if pairs else general_body
    return jax.shard_map(
        body, mesh=mesh, in_specs=placed, out_specs=P("rows", "blk"), check_vma=False
    )
```

time: 484 us -> 85.2 us (0.18)
  waiting for transfers between devices: 289 us -> 4.67 us
  blocking collectives: 124 us -> 0 us
  Pallas kernels: 0 us -> 72.3 us
  matrix products: 32 us -> 0 us
  between operations: 18.1 us -> 0.04 us
  other arithmetic: 11.9 us -> 1.56 us
  starting transfers between devices: 6.4 us -> 1.49 us
    psum x4 -> x0, waiting for transfers between devices: 220 us -> none  [statistics(): cross_gram, squares = lax.psum((cross_part, square_part), 'rows')]
    psum x4 -> x0, blocking collectives: 124 us -> none  [statistics(): cross_gram, squares = lax.psum((cross_part, square_part), 'rows')]
    pallas_call x0 -> x3, Pallas kernels: none -> 72.3 us  [the longest x1 46.9 us: pair_body(): pl.pallas_call(functools.partial(gram_kernel, n), out_shape=(jax.ShapeDty...]
    ppermute x6 -> x1, waiting for transfers between devices: 68.5 us -> 4.67 us  [pair_body(): far = lax.ppermute(late, 'blk', [(0, 1), (1, 0)])]
    dot_general x32 -> x0, matrix products: 32 us -> none  [the longest x4 9.02 us: statistics(): lax.dot_general(blocks[:, :BW], blocks[:, BW:], (((0,), (0,)), ((), ())),...]
    reduce_sum x8 -> x0, other arithmetic: 7.42 us -> none  [the longest x4 6.19 us: rotation(): magnitude = jnp.sqrt(jnp.sum(scaled * scaled) + epsilon)]
  transfers between devices with their start and end apart: 10 -> 1, of which waited for: 7 -> 1; matrix products, arithmetic and copies ran while one was open for 0% -> 0% of each run, Pallas kernels for 0% -> 21%
where the time goes in v1:
time: 85.2 us; the launch traced here: 84.9 us
  Pallas kernels  72.3 us (85%)
  local copies, waits for them, and re-layouts  4.83 us (6%)
  waiting for transfers between devices  4.67 us (5%)
  other arithmetic  1.56 us (2%)
  starting transfers between devices  1.49 us (2%)
    pallas_call x1, Pallas kernels, pair_body(): pl.pallas_call(functools.partial(gram_kernel, n), out_shape=(jax.ShapeDty...  46.9 us
    pallas_call x1, Pallas kernels, pair_body(): pl.pallas_call(chain_kernel, out_shape=(jax.ShapeDtypeStruct((width, widt...  17.6 us
    pallas_call x1, Pallas kernels, pair_body(): pl.pallas_call(apply_kernel, out_shape=jax.ShapeDtypeStruct((rows, width)...  7.73 us
    ppermute x1, waiting for transfers between devices, pair_body(): far = lax.ppermute(late, 'blk', [(0, 1), (1, 0)])  4.67 us
    unnamed x10, local copies, waits for them, and re-layouts  3.39 us
  transfers between devices with their start and end apart: 1, of which 1 were waited for; matrix products, arithmetic and copies ran while one was open for 0% of the time, Pallas kernels for 21%

profile of v1, /device:TPU:0, one launch (start us, length us, event | category | flops | bytes accessed | tf_op | source)
XLA Modules:
  0.0 84.9 jit_solution(6579217668632782270)
XLA Ops:
  0.0 0.0 copy-start
  0.0 0.8 convert_bitcast_fusion
  0.8 0.1 pad.1.clone
  0.9 0.1 pad.2.clone
  1.0 0.7 convert_element_type.6
  1.6 1.3 %constant_dynamic-slice_fusion = f32[1024,256]{1,0:T(8,128)S(1)} fusion(f32[2048,256]{1,0:T(8,128)} %x_ref.3, s32[]{:T(128)S(6)} %select_n.3), kind=kLoop, calls=%fused_computation.2 | loop fusion | bytes 2097156 | tf_op jit(solution)/shard_map/dynamic_slice | solution.py:374
  2.9 0.1 maximum_maximum_fusion.meta_ref
  3.0 0.0 copy-done
  3.0 46.9 %shard_map.37 = (f32[3,256,256]{2,1,0:T(8,128)S(1)}, f32[2,8,256]{2,1,0:T(8,128)S(1)}, f32[1024,256]{1,0:T(8,128)S(1)}) custom-call(f32[2048,256]{1,0:T(8,128)S(1)} %copy-done, f32[8,256]{1,0:T(8,128)S(1)} %maximum_maximum_fusion.meta_ref), custom_call_target="tpu_custom_call" | custom-call | tf_op jit(solution)/shard_map/pallas_call | solution.py:353
  50.0 0.0 copy-start.1
  50.0 1.0 %copy-done.1 = f32[1024,256]{1,0:T(8,128)} copy-done((f32[1024,256]{1,0:T(8,128)}, f32[1024,256]{1,0:T(8,128)S(1)}, u32[]{:S(2)}) %copy-start.1) | copy-done | bytes 1048600
  50.9 1.5 %collective-permute-start = (f32[1024,256]{1,0:T(8,128)S(1)}, f32[1024,256]{1,0:T(8,128)S(1)}, u32[]{:S(2)}, u32[]{:S(2)}) collective-permute-start(f32[1024,256]{1,0:T(8,128)S(1)} %constant_dynamic-slice_fusion), channel_id=1, source_target_pairs={{0,16},{16,0},{1,17},{17,1},{2,18},{18,2},{3,19},{19,3},{4,20},{20... | collective-permute-start | bytes 3145736 | tf_op jit(solution)/shard_map/ppermute | solution.py:376
  52.4 17.6 %shard_map.38 = (f32[256,256]{1,0:T(8,128)S(1)}, f32[256,256]{1,0:T(8,128)S(1)}) custom-call(f32[3,256,256]{2,1,0:T(8,128)S(1)} %get-tuple-element.15.gram_ref, f32[2,8,256]{2,1,0:T(8,128)S(1)} %get-tuple-element.16.meta_ref), custom_call_target="tpu_custom_call" | custom-call | flops 20000000000 | bytes 1572864 | tf_op jit(solution)/shard_map/pallas_call | solution.py:377
  70.0 0.0 copy-start.2
  70.0 0.7 copy-done.2
  70.7 0.0 copy-start.3
  70.7 0.7 copy-done.3
  71.4 4.7 %collective-permute-done.far_ref = f32[1024,256]{1,0:T(8,128)S(1)} collective-permute-done((f32[1024,256]{1,0:T(8,128)S(1)}, f32[1024,256]{1,0:T(8,128)S(1)}, u32[]{:S(2)}, u32[]{:S(2)}) %collective-permute-start) | collective-permute-done | bytes 1048608 | tf_op jit(solution)/shard_map/ppermute | solution.py:376
  76.1 0.0 copy-start.4
  76.1 1.0 %copy-done.4 = f32[1024,256]{1,0:T(8,128)} copy-done((f32[1024,256]{1,0:T(8,128)}, f32[1024,256]{1,0:T(8,128)S(1)}, u32[]{:S(2)}) %copy-start.4) | copy-done | bytes 1048600
  77.1 7.7 %shard_map.39 = f32[2048,256]{1,0:T(8,128)} custom-call(s32[1]{0:T(128)} %bitcast.where_ref, f32[2048,256]{1,0:T(8,128)} %x_ref.3, f32[1024,256]{1,0:T(8,128)} %copy-done.1, f32[1024,256]{1,0:T(8,128)} %copy-done.4, f32[256,256]{1,0:T(8,128)} %copy-done.2, f32[256,256]{1,0:T(8,128)} %copy-done.3), custom_call_target="tpu_custom_call" | custom-call | tf_op jit(solution)/shard_map/pallas_call | solution.py:393
  (1 shorter events, 0.0 us)
Async XLA Ops:
  0.0 3.0 %copy-start = (f32[2048,256]{1,0:T(8,128)S(1)}, f32[2048,256]{1,0:T(8,128)}, u32[]{:S(2)}) copy-start(f32[2048,256]{1,0:T(8,128)} %x_ref.3) | copy-start | bytes 6291460
  50.0 1.0 %copy-start.1 = (f32[1024,256]{1,0:T(8,128)}, f32[1024,256]{1,0:T(8,128)S(1)}, u32[]{:S(2)}) copy-start(f32[1024,256]{1,0:T(8,128)S(1)} %get-tuple-element.12.near_ref) | copy-start | bytes 3145732
  50.9 25.2 %collective-permute-start = (f32[1024,256]{1,0:T(8,128)S(1)}, f32[1024,256]{1,0:T(8,128)S(1)}, u32[]{:S(2)}, u32[]{:S(2)}) collective-permute-start(f32[1024,256]{1,0:T(8,128)S(1)} %constant_dynamic-slice_fusion), channel_id=1, source_target_pairs={{0,16},{16,0},{1,17},{17,1},{2,18},{18,2},{3,19},{19,3},{4,20},{20... | collective-permute-start | bytes 3145736 | tf_op jit(solution)/shard_map/ppermute | solution.py:376
  70.0 0.7 copy-start.2
  70.7 0.7 copy-start.3
  76.1 1.0 %copy-start.4 = (f32[1024,256]{1,0:T(8,128)}, f32[1024,256]{1,0:T(8,128)S(1)}, u32[]{:S(2)}) copy-start(f32[1024,256]{1,0:T(8,128)S(1)} %collective-permute-done.far_ref) | copy-start | bytes 3145732

commit v2 on v1

v2 whole, which is shorter than its diff:
```python
import functools

import jax
import jax.numpy as jnp
from jax import lax
from jax.experimental import pallas as pl
from jax.experimental.pallas import tpu as pltpu
from jax.sharding import PartitionSpec as P

BW = 128
ROUNDS = 4
NS_STEPS = 3
CHUNKS = 4
EXTRA = 1

epsilon = 1e-06
relaxation = 1.2

MESH = pl.DeviceIdType.MESH
ROWS_DIM = (((0,), (0,)), ((), ()))
PLAIN = (((1,), (0,)), ((), ()))
VMEM = pl.BlockSpec(memory_space=pltpu.VMEM)
ANY = pl.BlockSpec(memory_space=pl.ANY)


def from_behind(value, axis, by):
    peers = lax.axis_size(axis)
    return lax.ppermute(value, axis, [(i, (i + by) % peers) for i in range(peers)])


def rotation(cross_gram, squares, labels):
    left_scale = lax.rsqrt(squares[:BW] + epsilon)
    right_scale = lax.rsqrt(squares[BW:] + epsilon)
    grade_gap = jnp.abs(labels[:BW, None] - labels[None, BW:])
    scaled = cross_gram * left_scale[:, None] * right_scale[None, :] / (1.0 + grade_gap)
    magnitude = jnp.sqrt(jnp.sum(scaled * scaled) + epsilon)
    generator = relaxation * scaled / magnitude
    zeros_block = jnp.zeros_like(generator)
    upper_half = jnp.concatenate([zeros_block, generator], 1)
    lower_half = jnp.concatenate([-generator.T, zeros_block], 1)
    iterate = jnp.eye(2 * BW, dtype=generator.dtype) + jnp.concatenate([upper_half, lower_half], 0)
    for sweep in range(NS_STEPS):
        product = lax.dot_general(iterate, iterate, ROWS_DIM, precision=lax.Precision.HIGHEST)
        iterate = 1.5 * iterate - 0.5 * jnp.dot(iterate, product, precision=lax.Precision.HIGHEST)
    return iterate


def statistics(blocks):
    cross_part = lax.dot_general(
        blocks[:, :BW], blocks[:, BW:], ROWS_DIM, precision=lax.Precision.HIGHEST
    )
    square_part = jnp.sum(blocks * blocks, axis=0)
    return lax.psum((cross_part, square_part), "rows")


def assemble(first, incoming, staying):
    return jnp.where(
        first, jnp.concatenate([incoming, staying], -1), jnp.concatenate([staying, incoming], -1)
    )


def general_body(snapshots, grades, mover):
    blocks = snapshots
    labels = grades.astype(jnp.float32)
    for round_index in range(ROUNDS):
        cross_gram, squares = statistics(blocks)
        rotator = rotation(cross_gram, squares, labels)
        blocks = jnp.dot(blocks, rotator, precision=lax.Precision.HIGHEST)
        if round_index + 1 < ROUNDS:
            first = mover[round_index, 0] == 0
            move_label = jnp.where(first, labels[:BW], labels[BW:])
            stay_label = jnp.where(first, labels[BW:], labels[:BW])
            moving = jnp.where(first, blocks[:, :BW], blocks[:, BW:])
            staying = jnp.where(first, blocks[:, BW:], blocks[:, :BW])
            incoming, came_label = from_behind((moving, move_label), "blk", 1)
            blocks = assemble(first, incoming, staying)
            labels = assemble(first, came_label, stay_label)
    return blocks


def split(value):
    high = value.astype(jnp.bfloat16)
    return high, (value - high.astype(jnp.float32)).astype(jnp.bfloat16)


def dot_split(a, b, dims=PLAIN):
    (ah, al), (bh, bl) = a, b
    mul = functools.partial(lax.dot_general, dimension_numbers=dims, preferred_element_type=jnp.float32)
    return mul(ah, bh) + (mul(ah, bl) + mul(al, bh))


def dot3(a, b, dims=PLAIN):
    return dot_split(split(a), split(b), dims)


def dot6(a, b, dims=PLAIN):
    return lax.dot_general(
        a, b, dims, precision=lax.Precision.HIGHEST, preferred_element_type=jnp.float32
    )


def gram_kernel(
    n, x_ref, grade_ref, mover_ref, diag_ref, cross_ref, turn_ref, meta_out, near_ref,
    came, meta, meta_got, dpart, dgot, dmid, dnear, dfull, dother,
    cpart, cgot, cmid, cnear, cmine, cother, cfull,
    x_send, x_recv, rs_send, rs_recv, ag_send, ag_recv, sib_send, sib_recv, one_send, one_recv,
    local_sem,
):
    pos, me = lax.axis_index("blk"), lax.axis_index("rows")
    other = 1 - pos
    core, group = lax.rem(me, 2), me // 2
    groups = n // 2
    rows, width = x_ref.shape
    half = rows // 2
    piece = half // CHUNKS
    share = width // n
    partner, sibling = (other, me), (pos, me + 1 - 2 * core)
    peers = [None] + [lax.rem(group + k, groups) for k in range(1, groups)]

    barrier = pltpu.get_barrier_semaphore()
    for peer in peers[1:]:
        pl.semaphore_signal(barrier, inc=1, device_id=(pos, 2 * peer + core), device_id_type=MESH)
    for device in (partner, sibling):
        pl.semaphore_signal(barrier, inc=1, device_id=device, device_id_type=MESH)
    meta[...] = jnp.zeros_like(meta)
    meta[0:1, :] = grade_ref[...].astype(jnp.float32)
    for r in range(ROUNDS - 1):
        meta[r + 1:r + 2, :] = jnp.full((1, width), mover_ref[r, 0], jnp.int32).astype(jnp.float32)
    pl.semaphore_wait(barrier, groups + 1)

    def remote(src, dst, send, recv, device):
        copy = pltpu.make_async_remote_copy(
            src_ref=src, dst_ref=dst, send_sem=send, recv_sem=recv,
            device_id=device, device_id_type=MESH,
        )
        copy.start()
        return copy

    def swap(c):
        start = lax.rem(other * half + c * piece, rows)
        source = x_ref.at[pl.ds(pl.multiple_of(start, piece), piece)]
        return remote(source, came.at[pl.ds(c * piece, piece)], x_send.at[c], x_recv.at[c], partner)

    labels = remote(meta, meta_got, one_send.at[0], one_recv.at[0], partner)
    swaps = [swap(c) for c in range(CHUNKS)]

    def pair_up(part, got, which):
        return remote(part.at[1 - core], got, sib_send.at[which], sib_recv.at[which], sibling)

    def scatter(mid, near, which):
        return [
            remote(
                mid.at[peers[k]], near.at[k], rs_send.at[which, k], rs_recv.at[which, k],
                (pos, 2 * peers[k] + core),
            )
            for k in range(1, groups)
        ]

    def summed(mid, near, copies):
        total = mid[group]
        for k in range(1, groups):
            copies[k - 1].wait()
            total = total + near[k]
        return total

    def gather(full, which):
        return [
            remote(
                full.at[core, group], full.at[core, group], ag_send.at[which, k],
                ag_recv.at[which, k], (pos, 2 * peers[k] + core),
            )
            for k in range(1, groups)
        ]

    def hand_over(full, copies, which):
        for copy in copies:
            copy.wait()
        return remote(full.at[core], full.at[core], sib_send.at[which], sib_recv.at[which], sibling)

    def cross(c):
        swaps[c].wait()
        mine = x_ref[pl.ds(pl.multiple_of(pos * half + c * piece, piece), piece), :]
        theirs = came[c * piece:(c + 1) * piece, :]
        left = jnp.where(pos == 0, mine, theirs)
        right = jnp.where(pos == 0, theirs, mine)
        return dot3(left, right, ROWS_DIM)

    own = jnp.zeros((width, width), jnp.float32)
    for t in range(rows // piece):
        block = split(x_ref[t * piece:(t + 1) * piece, :])
        own = own + dot_split(block, block, ROWS_DIM)
    dpart[...] = own.reshape(2, groups, share, width)
    copy = pair_up(dpart, dgot, 0)
    total = cross(0)
    copy.wait()
    dmid[...] = dpart[core] + dgot[...]
    copies = scatter(dmid, dnear, 0)
    total = total + cross(1)
    dfull[core, group] = summed(dmid, dnear, copies)
    copies = gather(dfull, 0)
    total = total + cross(2)
    copy = hand_over(dfull, copies, 1)
    copy.wait()
    d_swap = remote(dfull, dother, one_send.at[1], one_recv.at[1], partner)
    for c in range(3, CHUNKS):
        total = total + cross(c)
    cpart[...] = total.reshape(2, groups, share, width)
    copy = pair_up(cpart, cgot, 2)
    copy.wait()
    cmid[...] = cpart[core] + cgot[...]
    copies = scatter(cmid, cnear, 1)
    cmine[...] = summed(cmid, cnear, copies)
    c_swap = remote(cmine, cother, one_send.at[2], one_recv.at[2], partner)
    late = [swap(c) for c in range(CHUNKS, CHUNKS + EXTRA)]
    c_swap.wait()
    cfull[core, group] = cmine[...] + cother[...]
    copies = gather(cfull, 1)

    labels.wait()
    meta_out[pos] = meta[...]
    meta_out[other] = meta_got[...]
    d_swap.wait()
    diag_ref[pos] = dfull[...].reshape(width, width)
    diag_ref[other] = dother[...].reshape(width, width)
    unit = eye(BW)
    generators = []
    for p in range(2):
        left_square = jnp.sum(diag_ref[p, :BW, :BW] * unit, axis=1, keepdims=True)
        right_square = jnp.sum(diag_ref[p, BW:, BW:] * unit, axis=0, keepdims=True)
        left_label = jnp.broadcast_to(meta_out[p, 0:1, :BW], (BW, BW)).T
        generators.append(
            polar(diag_ref[p, :BW, BW:], left_square, right_square, left_label, meta_out[p, 0:1, BW:])
        )
    for p, q in enumerate(rotations(generators)):
        turn_ref[p] = q
        diag_ref[p] = dot6(q, dot6(diag_ref[p], q), ROWS_DIM)

    copy = hand_over(cfull, copies, 3)
    copy.wait()
    cross_ref[...] = cfull[...].reshape(width, width)
    for copy in late:
        copy.wait()
    keep = pltpu.make_async_copy(came, near_ref, local_sem)
    keep.start()
    keep.wait()


def polar(cross_gram, left_square, right_square, left_label, right_label):
    left_scale = lax.rsqrt(left_square + epsilon)
    right_scale = lax.rsqrt(right_square + epsilon)
    scaled = cross_gram * left_scale * right_scale / (1.0 + jnp.abs(left_label - right_label))
    magnitude = jnp.sqrt(jnp.sum(scaled * scaled, keepdims=True) + epsilon)
    return relaxation * scaled / magnitude


def eye(n):
    return (
        lax.broadcasted_iota(jnp.int32, (n, n), 0) == lax.broadcasted_iota(jnp.int32, (n, n), 1)
    ).astype(jnp.float32)


def rotations(generators):
    unit = eye(BW)
    signs = [split(b) for b in generators]
    turned = [split(b.T) for b in generators]
    norm = []
    for b, bt in zip(signs, turned):
        norm.append(unit + dot_split(b, bt))
        norm.append(unit + dot_split(bt, b))
    gain = None
    for sweep in range(NS_STEPS):
        factor = [1.5 * unit - 0.5 * v for v in norm]
        cut = [split(f) for f in factor]
        last = sweep + 1 == NS_STEPS
        if last:
            edge = [dot_split(cut[2 * i], split(e)) for i, e in enumerate(edge)]
        else:
            parts = [split(v) for v in norm]
            inner = [2.25 * unit - 1.5 * v + 0.25 * dot_split(p, p) for v, p in zip(norm, parts)]
            norm = [dot_split(p, split(v)) for p, v in zip(parts, inner)]
        if gain is None:
            gain = factor
        else:
            gain = [dot_split(split(g), f) for g, f in zip(gain, cut)]
        if sweep + 2 == NS_STEPS:
            edge = [dot_split(split(gain[2 * i]), b) for i, b in enumerate(signs)]
    out = []
    for i, e in enumerate(edge):
        upper = jnp.concatenate([gain[2 * i], e], 1)
        lower = jnp.concatenate([-e.T, gain[2 * i + 1]], 1)
        out.append(jnp.concatenate([upper, lower], 0))
    return out


def chain_kernel(diag_ref, cross_ref, turn_ref, meta_ref, high_ref, low_ref, g, w, lab):
    pos = lax.axis_index("blk")
    width = 2 * BW
    small = eye(BW)
    between = dot6(turn_ref[0], dot6(cross_ref[...], turn_ref[1]), ROWS_DIM)
    for i in range(4):
        p, s = divmod(i, 2)
        rows = slice(s * BW, s * BW + BW)
        for j in range(4):
            q, t = divmod(j, 2)
            cols = slice(t * BW, t * BW + BW)
            if p == q:
                g[4 * i + j] = diag_ref[p, rows, cols]
            elif p == 0:
                g[4 * i + j] = between[rows, cols]
                g[4 * j + i] = between[rows, cols].T
        lab[i] = jnp.broadcast_to(meta_ref[p, 0:1, rows], (BW, BW))
        w[i] = jnp.zeros((2 * width, BW), jnp.float32)
        w[i, p * width:(p + 1) * width] = turn_ref[p, :, rows]

    def generator(a, b):
        left_square = jnp.sum(g[4 * a + a] * small, axis=1, keepdims=True)
        right_square = jnp.sum(g[4 * b + b] * small, axis=0, keepdims=True)
        return polar(g[4 * a + b], left_square, right_square, lab[a].T, lab[b])

    def step(slots, r):
        first = [jnp.max(meta_ref[p, r + 1:r + 2, :BW]) < 0.5 for p in range(2)]
        moving = [jnp.where(first[p], slots[p][0], slots[p][1]) for p in range(2)]
        staying = [jnp.where(first[p], slots[p][1], slots[p][0]) for p in range(2)]
        return [
            [
                jnp.where(first[p], moving[1 - p], staying[p]),
                jnp.where(first[p], staying[p], moving[1 - p]),
            ]
            for p in range(2)
        ]

    slots = step([[0, 1], [2, 3]], 0)
    for r in range(1, ROUNDS - 1):
        qs = rotations([generator(*slots[p]) for p in range(2)])
        for p, q in ((0, 0), (1, 1), (0, 1)):
            (a, b), (c, d) = slots[p], slots[q]
            upper = jnp.concatenate([g[4 * a + c], g[4 * a + d]], 1)
            lower = jnp.concatenate([g[4 * b + c], g[4 * b + d]], 1)
            block = jnp.concatenate([upper, lower], 0)
            block = dot6(qs[p], dot6(block, qs[q]), ROWS_DIM)
            for i, e in enumerate((a, b)):
                for j, f in enumerate((c, d)):
                    value = block[i * BW:(i + 1) * BW, j * BW:(j + 1) * BW]
                    g[4 * e + f] = value
                    if p != q:
                        g[4 * f + e] = value.T
        for p in range(2):
            a, b = slots[p]
            both = dot3(jnp.concatenate([w[a], w[b]], 1), qs[p])
            w[a] = both[:, :BW]
            w[b] = both[:, BW:]
        slots = step(slots, r)
    a = jnp.where(pos == 0, slots[0][0], slots[1][0])
    b = jnp.where(pos == 0, slots[0][1], slots[1][1])
    (q,) = rotations([generator(a, b)])
    cut = split(q)
    for p in range(2):
        rows = pl.ds(pl.multiple_of((pos if p == 0 else 1 - pos) * width, width), width)
        high, low = split(dot_split(split(jnp.concatenate([w[a, rows], w[b, rows]], 1)), cut))
        high_ref[p * width:(p + 1) * width] = high
        low_ref[p * width:(p + 1) * width] = low


def apply_kernel(first, count, tile, x_ref, partner_ref, high_ref, low_ref, *rest):
    out_ref, held, sems = rest[-3:]
    rows = x_ref.shape[0]
    blocks = rows // tile
    pos = lax.axis_index("blk")
    copies = []
    for i in range(count):
        there = pl.multiple_of(lax.rem(pos * CHUNKS + first + i, blocks) * tile, tile)
        here = slice(i * tile, i * tile + tile)
        data = split(jnp.concatenate([x_ref[pl.ds(there, tile), :], partner_ref[here, :]], 1))
        held[here, :] = dot_split(data, (high_ref[...], low_ref[...]))
        copies.append(
            pltpu.make_async_copy(held.at[here], out_ref.at[pl.ds(there, tile)], sems.at[i])
        )
        copies[-1].start()
    for copy in copies:
        copy.wait()


def apply(first, count, tile, snapshots, partner, high, low, out=None):
    rows, width = snapshots.shape
    extra = () if out is None else (out,)
    return pl.pallas_call(
        functools.partial(apply_kernel, first, count, tile),
        out_shape=jax.ShapeDtypeStruct((rows, width), jnp.float32),
        in_specs=[VMEM] * 4 + [ANY] * len(extra),
        out_specs=ANY,
        scratch_shapes=[
            pltpu.VMEM((count * tile, width), jnp.float32), pltpu.SemaphoreType.DMA((count,)),
        ],
        input_output_aliases={} if out is None else {4: 0},
        compiler_params=pltpu.CompilerParams(vmem_limit_bytes=24 * 1024 * 1024),
        cost_estimate=pl.CostEstimate(
            flops=count * tile * width * width * 48, bytes_accessed=count * tile * width * 16,
            transcendentals=0,
        ),
    )(snapshots, partner, high, low, *extra)


def pair_body(n, snapshots, grades, mover):
    rows, width = snapshots.shape
    share = width // n
    half = rows // 2
    tile = half // CHUNKS
    early = half + EXTRA * tile
    pos = lax.axis_index("blk")
    f32 = jnp.float32
    dma = pltpu.SemaphoreType.DMA
    whole = pltpu.VMEM((2, n // 2, share, width), f32)
    part = pltpu.VMEM((n // 2, share, width), f32)
    one = pltpu.VMEM((share, width), f32)
    square = jax.ShapeDtypeStruct((width, width), f32)
    squares = jax.ShapeDtypeStruct((2, width, width), f32)
    diag, cross, turn, meta, near = pl.pallas_call(
        functools.partial(gram_kernel, n),
        out_shape=(
            squares, square, squares,
            jax.ShapeDtypeStruct((2, 8, width), f32),
            jax.ShapeDtypeStruct((early, width), f32),
        ),
        in_specs=[VMEM, VMEM, pl.BlockSpec(memory_space=pltpu.SMEM)],
        out_specs=(VMEM, VMEM, VMEM, VMEM, ANY),
        scratch_shapes=[
            pltpu.VMEM((early, width), f32), pltpu.VMEM((8, width), f32), pltpu.VMEM((8, width), f32),
            whole, part, part, part, whole, whole,
            whole, part, part, part, one, one, whole,
            dma((CHUNKS + EXTRA,)), dma((CHUNKS + EXTRA,)),
            dma((2, n // 2)), dma((2, n // 2)), dma((2, n // 2)), dma((2, n // 2)),
            dma((4,)), dma((4,)), dma((3,)), dma((3,)), dma,
        ],
        compiler_params=pltpu.CompilerParams(
            collective_id=0, has_side_effects=True, vmem_limit_bytes=40 * 1024 * 1024
        ),
    )(snapshots, grades.reshape(1, width), mover)
    late = lax.dynamic_slice_in_dim(snapshots, pos * half + EXTRA * tile, rows - early, 0)
    late, cross = lax.optimization_barrier((late, cross))
    far = lax.ppermute(late, "blk", [(0, 1), (1, 0)])
    high, low = pl.pallas_call(
        chain_kernel,
        out_shape=(jax.ShapeDtypeStruct((2 * width, width), jnp.bfloat16),) * 2,
        in_specs=[VMEM] * 4,
        out_specs=(VMEM, VMEM),
        scratch_shapes=[
            pltpu.VMEM((16, BW, BW), f32),
            pltpu.VMEM((4, 2 * width, BW), f32),
            pltpu.VMEM((4, BW, BW), f32),
        ],
        compiler_params=pltpu.CompilerParams(vmem_limit_bytes=32 * 1024 * 1024),
        cost_estimate=pl.CostEstimate(
            flops=15 * 10**9, bytes_accessed=4 * width * width * 8, transcendentals=0
        ),
    )(diag, cross, turn, meta)
    done = CHUNKS + EXTRA
    out = apply(0, done, tile, snapshots, near, high, low)
    return apply(done, CHUNKS - EXTRA, tile, snapshots, far, high, low, out)


def solution(mesh):
    placed = (P("rows", "blk"), P("blk"), P(None, "blk"))
    n = mesh.shape["rows"]
    pairs = mesh.shape["blk"] == 2 and n % 2 == 0 and (2 * BW) % (8 * n) == 0
    body = functools.partial(pair_body, n) if pairs else general_body
    return jax.shard_map(
        body, mesh=mesh, in_specs=placed, out_specs=P("rows", "blk"), check_vma=False
    )
```

time: 85.2 us -> 73.7 us (0.87)
  Pallas kernels: 72.3 us -> 64.7 us
  waiting for transfers between devices: 4.67 us -> 2.23 us
  other arithmetic: 1.56 us -> 0 us
    pallas_call x3 -> x4, Pallas kernels: 72.3 us -> 64.7 us  [the longest x1 47.3 us: pair_body(): pl.pallas_call(functools.partial(gram_kernel, n), out_shape=(squares, squ...]
    ppermute x1, waiting for transfers between devices: 4.67 us -> 2.23 us  [pair_body(): far = lax.ppermute(late, 'blk', [(0, 1), (1, 0)])]
    unnamed x10 -> x5, local copies, waits for them, and re-layouts: 3.39 us -> 3.01 us
  transfers between devices with their start and end apart: 1 -> 1, of which waited for: 1 -> 1; matrix products, arithmetic and copies ran while one was open for 0% -> 0% of each run, Pallas kernels for 21% -> 22%
where the time goes in v2:
time: 73.7 us; the launch traced here: 73.5 us
  Pallas kernels  64.7 us (88%)
  local copies, waits for them, and re-layouts  4.19 us (6%)
  waiting for transfers between devices  2.23 us (3%)
  starting transfers between devices  2.19 us (3%)
    pallas_call x1, Pallas kernels, pair_body(): pl.pallas_call(functools.partial(gram_kernel, n), out_shape=(squares, squ...  47.3 us
    pallas_call x1, Pallas kernels, pair_body(): pl.pallas_call(chain_kernel, out_shape=(jax.ShapeDtypeStruct((2 * width,...  13.7 us
    pallas_call x2, Pallas kernels, apply(): pl.pallas_call(functools.partial(apply_kernel, first, count, tile), out_s...  3.66 us
    unnamed x5, local copies, waits for them, and re-layouts  3.01 us
    ppermute x1, waiting for transfers between devices, pair_body(): far = lax.ppermute(late, 'blk', [(0, 1), (1, 0)])  2.23 us
    ppermute x1, starting transfers between devices, pair_body(): far = lax.ppermute(late, 'blk', [(0, 1), (1, 0)])  2.19 us
  transfers between devices with their start and end apart: 1, of which 1 were waited for; matrix products, arithmetic and copies ran while one was open for 0% of the time, Pallas kernels for 22%

profile of v2, /device:TPU:0, one launch (start us, length us, event | category | flops | bytes accessed | tf_op | source)
XLA Modules:
  0.0 73.5 jit_solution(8254517874881467701)
XLA Ops:
  0.0 0.7 %copy.5.mover_ref = s32[3,1]{1,0:T(4,128)S(1)} copy(s32[3,1]{0,1:T(1,128)} %param.5) | data formatting | bytes 24 | tf_op args[2]
  0.7 1.2 %constant_dynamic-slice_fusion = f32[768,256]{1,0:T(8,128)S(1)} fusion(f32[2048,256]{1,0:T(8,128)} %x_ref.5, s32[]{:T(128)S(6)} %select_n.3), kind=kLoop, calls=%fused_computation | loop fusion | bytes 1572868 | tf_op jit(solution)/shard_map/dynamic_slice | solution.py:438
  1.9 0.0 copy-start
  1.9 1.6 %copy-done = f32[2048,256]{1,0:T(8,128)S(1)} copy-done((f32[2048,256]{1,0:T(8,128)S(1)}, f32[2048,256]{1,0:T(8,128)}, u32[]{:S(2)}) %copy-start) | copy-done | bytes 2097176
  3.5 0.0 copy-start.1
  3.5 0.7 copy-done.1
  4.2 47.3 %shard_map.37 = (f32[2,256,256]{2,1,0:T(8,128)S(1)}, f32[256,256]{1,0:T(8,128)S(1)}, f32[2,256,256]{2,1,0:T(8,128)S(1)}, f32[2,8,256]{2,1,0:T(8,128)S(1)}, f32[1280,256]{1,0:T(8,128)S(1)}) custom-call(f32[2048,256]{1,0:T(8,128)S(1)} %copy-done, s32[1,256]{1,0:T(1,128)S(1)} %bitcast.1, s32[3,1]{1,0:T(4,128)S(1)} %copy.5.mover_ref), custom_call_target="tpu_custom_call" | custom-call | tf_op jit(solution)/shard_map/pallas_call | solution.py:417
  51.5 2.2 %collective-permute-start = (f32[768,256]{1,0:T(8,128)S(1)}, f32[768,256]{1,0:T(8,128)S(1)}, u32[]{:S(2)}, u32[]{:S(2)}) collective-permute-start(f32[768,256]{1,0:T(8,128)S(1)} %constant_dynamic-slice_fusion), channel_id=1, source_target_pairs={{0,16},{16,0},{1,17},{17,1},{2,18},{18,2},{3,19},{19,3},{4,20},{20... | collective-permute-start | bytes 2359304 | tf_op jit(solution)/shard_map/ppermute | solution.py:440
  53.7 13.7 %shard_map.38 = (bf16[512,256]{1,0:T(8,128)(2,1)S(1)}, bf16[512,256]{1,0:T(8,128)(2,1)S(1)}) custom-call(f32[2,256,256]{2,1,0:T(8,128)S(1)} %get-tuple-element.16.diag_ref, f32[256,256]{1,0:T(8,128)S(1)} %get-tuple-element.17.cross_ref, f32[2,256,256]{2,1,0:T(8,128)S(1)} %get-tuple-element.18.turn_ref, f32[2,8,256]{2,1,0:T(8,128)S(1)} %get-tuple-element.19.meta_ref), custom_call_target="tpu_custom_call" | custom-call | flops 15000000512 | bytes 2097152 | tf_op jit(solution)/shard_map/pallas_call | solution.py:441
  67.5 2.1 %shard_map.39.rest_0_ = f32[2048,256]{1,0:T(8,128)} custom-call(f32[2048,256]{1,0:T(8,128)S(1)} %copy-done, f32[1280,256]{1,0:T(8,128)S(1)} %get-tuple-element.22.partner_ref, bf16[512,256]{1,0:T(8,128)(2,1)S(1)} %get-tuple-element.20.high_ref, bf16[512,256]{1,0:T(8,128)(2,1)S(1)} %get-tuple-element.21.low_ref), custom_call_target="tpu_custom_call" | custom-call | flops 4026531840 | bytes 5242880 | tf_op jit(solution)/shard_map/pallas_call | solution.py:386
  69.6 2.2 %collective-permute-done.partner_ref = f32[768,256]{1,0:T(8,128)S(1)} collective-permute-done((f32[768,256]{1,0:T(8,128)S(1)}, f32[768,256]{1,0:T(8,128)S(1)}, u32[]{:S(2)}, u32[]{:S(2)}) %collective-permute-start) | collective-permute-done | bytes 786464 | tf_op jit(solution)/shard_map/ppermute | solution.py:440
  71.8 1.6 %shard_map.40 = f32[2048,256]{1,0:T(8,128)} custom-call(f32[2048,256]{1,0:T(8,128)S(1)} %copy-done, f32[768,256]{1,0:T(8,128)S(1)} %collective-permute-done.partner_ref, bf16[512,256]{1,0:T(8,128)(2,1)S(1)} %get-tuple-element.20.high_ref, bf16[512,256]{1,0:T(8,128)(2,1)S(1)} %get-tuple-element.21.low_ref, ...), custom_call_target="tpu_custom_call", output_to_operand_aliasing={{}: (4, {})} | custom-call | flops 2415919104 | bytes 3145728 | tf_op jit(solution)/shard_map/pallas_call | solution.py:386
Async XLA Ops:
  1.9 1.6 %copy-start = (f32[2048,256]{1,0:T(8,128)S(1)}, f32[2048,256]{1,0:T(8,128)}, u32[]{:S(2)}) copy-start(f32[2048,256]{1,0:T(8,128)} %x_ref.5) | copy-start | bytes 6291460
  3.5 0.7 copy-start.1
  51.5 20.3 %collective-permute-start = (f32[768,256]{1,0:T(8,128)S(1)}, f32[768,256]{1,0:T(8,128)S(1)}, u32[]{:S(2)}, u32[]{:S(2)}) collective-permute-start(f32[768,256]{1,0:T(8,128)S(1)} %constant_dynamic-slice_fusion), channel_id=1, source_target_pairs={{0,16},{16,0},{1,17},{17,1},{2,18},{18,2},{3,19},{19,3},{4,20},{20... | collective-permute-start | bytes 2359304 | tf_op jit(solution)/shard_map/ppermute | solution.py:440

commit v3 on v2

--- a/solution.py
+++ b/solution.py
@@ -10,8 +10,10 @@
 BW = 128
 ROUNDS = 4
 NS_STEPS = 3
-CHUNKS = 4
-EXTRA = 1
+CHUNKS = 8
+EXTRA = 4
+SOON = 1
+TALL = 2
 
 epsilon = 1e-06
 relaxation = 1.2
@@ -21,6 +23,7 @@
 PLAIN = (((1,), (0,)), ((), ()))
 VMEM = pl.BlockSpec(memory_space=pltpu.VMEM)
 ANY = pl.BlockSpec(memory_space=pl.ANY)
+HBM = pl.BlockSpec(memory_space=pltpu.HBM)
 
 
 def from_behind(value, axis, by):
@@ -100,11 +103,11 @@
 
 
 def gram_kernel(
-    n, x_ref, grade_ref, mover_ref, diag_ref, cross_ref, turn_ref, meta_out, near_ref,
-    came, meta, meta_got, dpart, dgot, dmid, dnear, dfull, dother,
+    n, x_hbm, grade_ref, mover_ref, diag_ref, cross_ref, turn_ref, meta_out, near_ref, late_ref,
+    x_ref, grade, came, meta, meta_got, dpart, dgot, dmid, dnear, dfull, dother,
     cpart, cgot, cmid, cnear, cmine, cother, cfull,
     x_send, x_recv, rs_send, rs_recv, ag_send, ag_recv, sib_send, sib_recv, one_send, one_recv,
-    local_sem,
+    load_sem, near_sem, side_sem,
 ):
     pos, me = lax.axis_index("blk"), lax.axis_index("rows")
     other = 1 - pos
@@ -117,13 +120,22 @@
     partner, sibling = (other, me), (pos, me + 1 - 2 * core)
     peers = [None] + [lax.rem(group + k, groups) for k in range(1, groups)]
 
+    grade_load = pltpu.make_async_copy(grade_ref, grade, side_sem.at[0])
+    grade_load.start()
+    loads = []
+    for t in range(rows // piece):
+        at = pl.ds(t * piece, piece)
+        loads.append(pltpu.make_async_copy(x_hbm.at[at], x_ref.at[at], load_sem.at[t]))
+        loads[-1].start()
+
     barrier = pltpu.get_barrier_semaphore()
     for peer in peers[1:]:
         pl.semaphore_signal(barrier, inc=1, device_id=(pos, 2 * peer + core), device_id_type=MESH)
     for device in (partner, sibling):
         pl.semaphore_signal(barrier, inc=1, device_id=device, device_id_type=MESH)
     meta[...] = jnp.zeros_like(meta)
-    meta[0:1, :] = grade_ref[...].astype(jnp.float32)
+    grade_load.wait()
+    meta[0:1, :] = grade[...].astype(jnp.float32)
     for r in range(ROUNDS - 1):
         meta[r + 1:r + 2, :] = jnp.full((1, width), mover_ref[r, 0], jnp.int32).astype(jnp.float32)
     pl.semaphore_wait(barrier, groups + 1)
@@ -138,7 +150,7 @@
 
     def swap(c):
         start = lax.rem(other * half + c * piece, rows)
-        source = x_ref.at[pl.ds(pl.multiple_of(start, piece), piece)]
+        source = x_hbm.at[pl.ds(pl.multiple_of(start, piece), piece)]
         return remote(source, came.at[pl.ds(c * piece, piece)], x_send.at[c], x_recv.at[c], partner)
 
     labels = remote(meta, meta_got, one_send.at[0], one_recv.at[0], partner)
@@ -177,8 +189,16 @@
             copy.wait()
         return remote(full.at[core], full.at[core], sib_send.at[which], sib_recv.at[which], sibling)
 
+    kept = []
+
+    def keep(c):
+        at = pl.ds(c * piece, piece)
+        kept.append(pltpu.make_async_copy(came.at[at], near_ref.at[at], near_sem.at[c]))
+        kept[-1].start()
+
     def cross(c):
         swaps[c].wait()
+        keep(c)
         mine = x_ref[pl.ds(pl.multiple_of(pos * half + c * piece, piece), piece), :]
         theirs = came[c * piece:(c + 1) * piece, :]
         left = jnp.where(pos == 0, mine, theirs)
@@ -187,62 +207,71 @@
 
     own = jnp.zeros((width, width), jnp.float32)
     for t in range(rows // piece):
+        loads[t].wait()
         block = split(x_ref[t * piece:(t + 1) * piece, :])
         own = own + dot_split(block, block, ROWS_DIM)
     dpart[...] = own.reshape(2, groups, share, width)
     copy = pair_up(dpart, dgot, 0)
-    total = cross(0)
+    begin = pl.multiple_of(pos * half + EXTRA * piece, piece)
+    aside = pltpu.make_async_copy(
+        x_ref.at[pl.ds(begin, half - EXTRA * piece)], late_ref, side_sem.at[1]
+    )
+    aside.start()
+    total = cross(0) + cross(1)
     copy.wait()
     dmid[...] = dpart[core] + dgot[...]
     copies = scatter(dmid, dnear, 0)
-    total = total + cross(1)
+    total = total + cross(2)
     dfull[core, group] = summed(dmid, dnear, copies)
     copies = gather(dfull, 0)
-    total = total + cross(2)
+    total = total + cross(3) + cross(4)
     copy = hand_over(dfull, copies, 1)
     copy.wait()
     d_swap = remote(dfull, dother, one_send.at[1], one_recv.at[1], partner)
-    for c in range(3, CHUNKS):
+    late = [swap(c) for c in range(CHUNKS, CHUNKS + SOON)]
+    for c in range(5, CHUNKS):
         total = total + cross(c)
     cpart[...] = total.reshape(2, groups, share, width)
     copy = pair_up(cpart, cgot, 2)
+    diag_ref[pos] = dfull[...].reshape(width, width)
+    labels.wait()
+    meta_out[pos] = meta[...]
+    meta_out[other] = meta_got[...]
     copy.wait()
     cmid[...] = cpart[core] + cgot[...]
     copies = scatter(cmid, cnear, 1)
+    unit = eye(BW)
+
+    def begin_round(p):
+        diag = diag_ref[p]
+        left_square = jnp.sum(diag[:BW, :BW] * unit, axis=1, keepdims=True)
+        right_square = jnp.sum(diag[BW:, BW:] * unit, axis=0, keepdims=True)
+        left_label = jnp.broadcast_to(meta_out[p, 0:1, :BW], (BW, BW)).T
+        (q,) = rotations(
+            [polar(diag[:BW, BW:], left_square, right_square, left_label, meta_out[p, 0:1, BW:])]
+        )
+        turn_ref[p] = q
+        diag_ref[p] = dot6(q, dot6(diag, q), ROWS_DIM)
+
+    begin_round(pos)
     cmine[...] = summed(cmid, cnear, copies)
     c_swap = remote(cmine, cother, one_send.at[2], one_recv.at[2], partner)
-    late = [swap(c) for c in range(CHUNKS, CHUNKS + EXTRA)]
+    late += [swap(c) for c in range(CHUNKS + SOON, CHUNKS + EXTRA)]
+    d_swap.wait()
+    diag_ref[other] = dother[...].reshape(width, width)
     c_swap.wait()
     cfull[core, group] = cmine[...] + cother[...]
     copies = gather(cfull, 1)
-
-    labels.wait()
-    meta_out[pos] = meta[...]
-    meta_out[other] = meta_got[...]
-    d_swap.wait()
-    diag_ref[pos] = dfull[...].reshape(width, width)
-    diag_ref[other] = dother[...].reshape(width, width)
-    unit = eye(BW)
-    generators = []
-    for p in range(2):
-        left_square = jnp.sum(diag_ref[p, :BW, :BW] * unit, axis=1, keepdims=True)
-        right_square = jnp.sum(diag_ref[p, BW:, BW:] * unit, axis=0, keepdims=True)
-        left_label = jnp.broadcast_to(meta_out[p, 0:1, :BW], (BW, BW)).T
-        generators.append(
-            polar(diag_ref[p, :BW, BW:], left_square, right_square, left_label, meta_out[p, 0:1, BW:])
-        )
-    for p, q in enumerate(rotations(generators)):
-        turn_ref[p] = q
-        diag_ref[p] = dot6(q, dot6(diag_ref[p], q), ROWS_DIM)
-
+    begin_round(other)
     copy = hand_over(cfull, copies, 3)
+    for c in range(EXTRA):
+        late[c].wait()
+        keep(CHUNKS + c)
     copy.wait()
     cross_ref[...] = cfull[...].reshape(width, width)
-    for copy in late:
+    aside.wait()
+    for copy in kept:
         copy.wait()
-    keep = pltpu.make_async_copy(came, near_ref, local_sem)
-    keep.start()
-    keep.wait()
 
 
 def polar(cross_gram, left_square, right_square, left_label, right_label):
@@ -292,7 +321,7 @@
     return out
 
 
-def chain_kernel(diag_ref, cross_ref, turn_ref, meta_ref, high_ref, low_ref, g, w, lab):
+def chain_kernel(diag_ref, cross_ref, turn_ref, meta_ref, high_ref, low_ref, g, w, lab, squares):
     pos = lax.axis_index("blk")
     width = 2 * BW
     small = eye(BW)
@@ -312,9 +341,13 @@
         w[i] = jnp.zeros((2 * width, BW), jnp.float32)
         w[i, p * width:(p + 1) * width] = turn_ref[p, :, rows]
 
-    def generator(a, b):
-        left_square = jnp.sum(g[4 * a + a] * small, axis=1, keepdims=True)
-        right_square = jnp.sum(g[4 * b + b] * small, axis=0, keepdims=True)
+    def generator(a, b, known=False):
+        if known:
+            left_square = jnp.broadcast_to(squares[a, 0:1], (BW, BW)).T
+            right_square = squares[b, 0:1]
+        else:
+            left_square = jnp.sum(g[4 * a + a] * small, axis=1, keepdims=True)
+            right_square = jnp.sum(g[4 * b + b] * small, axis=0, keepdims=True)
         return polar(g[4 * a + b], left_square, right_square, lab[a].T, lab[b])
 
     def step(slots, r):
@@ -332,12 +365,19 @@
     slots = step([[0, 1], [2, 3]], 0)
     for r in range(1, ROUNDS - 1):
         qs = rotations([generator(*slots[p]) for p in range(2)])
+        last = r + 2 == ROUNDS
         for p, q in ((0, 0), (1, 1), (0, 1)):
             (a, b), (c, d) = slots[p], slots[q]
             upper = jnp.concatenate([g[4 * a + c], g[4 * a + d]], 1)
             lower = jnp.concatenate([g[4 * b + c], g[4 * b + d]], 1)
             block = jnp.concatenate([upper, lower], 0)
-            block = dot6(qs[p], dot6(block, qs[q]), ROWS_DIM)
+            block = dot6(block, qs[q])
+            if last and p == q:
+                square = jnp.sum(qs[p] * block, axis=0, keepdims=True)
+                squares[a] = jnp.broadcast_to(square[:, :BW], (8, BW))
+                squares[b] = jnp.broadcast_to(square[:, BW:], (8, BW))
+                continue
+            block = dot6(qs[p], block, ROWS_DIM)
             for i, e in enumerate((a, b)):
                 for j, f in enumerate((c, d)):
                     value = block[i * BW:(i + 1) * BW, j * BW:(j + 1) * BW]
@@ -352,7 +392,7 @@
         slots = step(slots, r)
     a = jnp.where(pos == 0, slots[0][0], slots[1][0])
     b = jnp.where(pos == 0, slots[0][1], slots[1][1])
-    (q,) = rotations([generator(a, b)])
+    (q,) = rotations([generator(a, b, True)])
     cut = split(q)
     for p in range(2):
         rows = pl.ds(pl.multiple_of((pos if p == 0 else 1 - pos) * width, width), width)
@@ -368,7 +408,7 @@
     pos = lax.axis_index("blk")
     copies = []
     for i in range(count):
-        there = pl.multiple_of(lax.rem(pos * CHUNKS + first + i, blocks) * tile, tile)
+        there = pl.multiple_of(lax.rem(pos * (blocks // 2) + first + i, blocks) * tile, tile)
         here = slice(i * tile, i * tile + tile)
         data = split(jnp.concatenate([x_ref[pl.ds(there, tile), :], partner_ref[here, :]], 1))
         held[here, :] = dot_split(data, (high_ref[...], low_ref[...]))
@@ -404,9 +444,9 @@
     rows, width = snapshots.shape
     share = width // n
     half = rows // 2
-    tile = half // CHUNKS
-    early = half + EXTRA * tile
-    pos = lax.axis_index("blk")
+    piece = half // CHUNKS
+    early = half + EXTRA * piece
+    tile = TALL * piece
     f32 = jnp.float32
     dma = pltpu.SemaphoreType.DMA
     whole = pltpu.VMEM((2, n // 2, share, width), f32)
@@ -414,29 +454,30 @@
     one = pltpu.VMEM((share, width), f32)
     square = jax.ShapeDtypeStruct((width, width), f32)
     squares = jax.ShapeDtypeStruct((2, width, width), f32)
-    diag, cross, turn, meta, near = pl.pallas_call(
+    diag, cross, turn, meta, near, late = pl.pallas_call(
         functools.partial(gram_kernel, n),
         out_shape=(
             squares, square, squares,
             jax.ShapeDtypeStruct((2, 8, width), f32),
             jax.ShapeDtypeStruct((early, width), f32),
+            jax.ShapeDtypeStruct((rows - early, width), f32),
         ),
-        in_specs=[VMEM, VMEM, pl.BlockSpec(memory_space=pltpu.SMEM)],
-        out_specs=(VMEM, VMEM, VMEM, VMEM, ANY),
+        in_specs=[HBM, HBM, pl.BlockSpec(memory_space=pltpu.SMEM)],
+        out_specs=(VMEM, VMEM, VMEM, VMEM, ANY, ANY),
         scratch_shapes=[
+            pltpu.VMEM((rows, width), f32), pltpu.VMEM((1, width), jnp.int32),
             pltpu.VMEM((early, width), f32), pltpu.VMEM((8, width), f32), pltpu.VMEM((8, width), f32),
             whole, part, part, part, whole, whole,
             whole, part, part, part, one, one, whole,
             dma((CHUNKS + EXTRA,)), dma((CHUNKS + EXTRA,)),
             dma((2, n // 2)), dma((2, n // 2)), dma((2, n // 2)), dma((2, n // 2)),
-            dma((4,)), dma((4,)), dma((3,)), dma((3,)), dma,
+            dma((4,)), dma((4,)), dma((3,)), dma((3,)),
+            dma((2 * CHUNKS,)), dma((CHUNKS + EXTRA,)), dma((2,)),
         ],
         compiler_params=pltpu.CompilerParams(
             collective_id=0, has_side_effects=True, vmem_limit_bytes=40 * 1024 * 1024
         ),
     )(snapshots, grades.reshape(1, width), mover)
-    late = lax.dynamic_slice_in_dim(snapshots, pos * half + EXTRA * tile, rows - early, 0)
-    late, cross = lax.optimization_barrier((late, cross))
     far = lax.ppermute(late, "blk", [(0, 1), (1, 0)])
     high, low = pl.pallas_call(
         chain_kernel,
@@ -447,15 +488,16 @@
             pltpu.VMEM((16, BW, BW), f32),
             pltpu.VMEM((4, 2 * width, BW), f32),
             pltpu.VMEM((4, BW, BW), f32),
+            pltpu.VMEM((4, 8, BW), f32),
         ],
         compiler_params=pltpu.CompilerParams(vmem_limit_bytes=32 * 1024 * 1024),
         cost_estimate=pl.CostEstimate(
             flops=15 * 10**9, bytes_accessed=4 * width * width * 8, transcendentals=0
         ),
     )(diag, cross, turn, meta)
-    done = CHUNKS + EXTRA
+    done = early // tile
     out = apply(0, done, tile, snapshots, near, high, low)
-    return apply(done, CHUNKS - EXTRA, tile, snapshots, far, high, low, out)
+    return apply(done, rows // tile - done, tile, snapshots, far, high, low, out)
 
 
 def solution(mesh):

time: 73.7 us -> 72.6 us (0.985)
  Pallas kernels: 64.7 us -> 68.3 us
  waiting for transfers between devices: 2.23 us -> 0.01 us
  starting transfers between devices: 2.19 us -> 0.84 us
  local copies, waits for them, and re-layouts: 4.19 us -> 3.01 us
    pallas_call x1, Pallas kernels: 47.3 us -> 52.6 us  [pair_body(): pl.pallas_call(functools.partial(gram_kernel, n), out_shape=(squares, squ...]
    ppermute x1, waiting for transfers between devices: 2.23 us -> 0.01 us  [pair_body(): far = lax.ppermute(late, 'blk', [(0, 1), (1, 0)])]
    pallas_call x1, Pallas kernels: 13.7 us -> 12 us  [pair_body(): pl.pallas_call(chain_kernel, out_shape=(jax.ShapeDtypeStruct((2 * width,...]
    ppermute x1, starting transfers between devices: 2.19 us -> 0.84 us  [pair_body(): far = lax.ppermute(late, 'blk', [(0, 1), (1, 0)])]
    dynamic_slice x1 -> x0, local copies, waits for them, and re-layouts: 1.18 us -> none  [pair_body(): lax.dynamic_slice_in_dim(snapshots, pos * half + EXTRA * tile, rows - ear...]
  transfers between devices with their start and end apart: 1 -> 1, of which waited for: 1 -> 0; matrix products, arithmetic and copies ran while one was open for 0% -> 0% of each run, Pallas kernels for 22% -> 20%
where the time goes in v3:
time: 72.6 us; the launch traced here: 72.4 us
  Pallas kernels  68.3 us (94%)
  local copies, waits for them, and re-layouts  3.01 us (4%)
  starting transfers between devices  0.84 us (1%)
    pallas_call x1, Pallas kernels, pair_body(): pl.pallas_call(functools.partial(gram_kernel, n), out_shape=(squares, squ...  52.6 us
    pallas_call x1, Pallas kernels, pair_body(): pl.pallas_call(chain_kernel, out_shape=(jax.ShapeDtypeStruct((2 * width,...  12 us
    pallas_call x2, Pallas kernels, apply(): pl.pallas_call(functools.partial(apply_kernel, first, count, tile), out_s...  3.73 us
    unnamed x5, local copies, waits for them, and re-layouts  3.01 us
  transfers between devices with their start and end apart: 1, of which 0 were waited for; matrix products, arithmetic and copies ran while one was open for 0% of the time, Pallas kernels for 20%

profile of v3, /device:TPU:0, one launch (start us, length us, event | category | flops | bytes accessed | tf_op | source)
XLA Modules:
  0.0 72.4 jit_solution(10953653772510974947)
XLA Ops:
  0.0 0.7 %copy.5.mover_ref = s32[3,1]{1,0:T(4,128)S(1)} copy(s32[3,1]{0,1:T(1,128)} %param.5) | data formatting | bytes 24 | tf_op args[2]
  0.7 0.0 copy-start
  0.7 1.6 %copy-done = f32[2048,256]{1,0:T(8,128)S(1)} copy-done((f32[2048,256]{1,0:T(8,128)S(1)}, f32[2048,256]{1,0:T(8,128)}, u32[]{:S(2)}) %copy-start) | copy-done | bytes 2097176
  2.3 0.0 copy-start.1
  2.3 0.7 copy-done.1
  3.0 52.6 %shard_map.37 = (f32[2,256,256]{2,1,0:T(8,128)S(1)}, f32[256,256]{1,0:T(8,128)S(1)}, f32[2,256,256]{2,1,0:T(8,128)S(1)}, f32[2,8,256]{2,1,0:T(8,128)S(1)}, f32[1...) custom-call(f32[2048,256]{1,0:T(8,128)S(1)} %copy-done, s32[1,256]{1,0:T(1,128)S(1)} %bitcast.1, s32[3,1]{1,0:T(4,128)S(1)} %copy.5.mover_ref), custom_call_target="tpu_custom_call" | custom-call | tf_op jit(solution)/shard_map/pallas_call | solution.py:457
  55.7 0.8 %collective-permute-start = (f32[512,256]{1,0:T(8,128)S(1)}, f32[512,256]{1,0:T(8,128)S(1)}, u32[]{:S(2)}, u32[]{:S(2)}) collective-permute-start(f32[512,256]{1,0:T(8,128)S(1)} %get-tuple-element.13), channel_id=1, source_target_pairs={{0,16},{16,0},{1,17},{17,1},{2,18},{18,2},{3,19},{19,3},{4,20},{20... | collective-permute-start | bytes 1572872 | tf_op jit(solution)/shard_map/ppermute | solution.py:481
  56.5 12.0 %shard_map.38 = (bf16[512,256]{1,0:T(8,128)(2,1)S(1)}, bf16[512,256]{1,0:T(8,128)(2,1)S(1)}) custom-call(f32[2,256,256]{2,1,0:T(8,128)S(1)} %get-tuple-element.14.diag_ref, f32[256,256]{1,0:T(8,128)S(1)} %get-tuple-element.15.cross_ref, f32[2,256,256]{2,1,0:T(8,128)S(1)} %get-tuple-element.16.turn_ref, f32[2,8,256]{2,1,0:T(8,128)S(1)} %get-tuple-element.17.meta_ref), custom_call_target="tpu_custom_call" | custom-call | flops 15000000512 | bytes 2097152 | tf_op jit(solution)/shard_map/pallas_call | solution.py:482
  68.5 2.3 %shard_map.39.rest_0_ = f32[2048,256]{1,0:T(8,128)} custom-call(f32[2048,256]{1,0:T(8,128)S(1)} %copy-done, f32[1536,256]{1,0:T(8,128)S(1)} %get-tuple-element.20.partner_ref, bf16[512,256]{1,0:T(8,128)(2,1)S(1)} %get-tuple-element.18.high_ref, bf16[512,256]{1,0:T(8,128)(2,1)S(1)} %get-tuple-element.19.low_ref), custom_call_target="tpu_custom_call" | custom-call | flops 4831838208 | bytes 6291456 | tf_op jit(solution)/shard_map/pallas_call | solution.py:426
  70.8 0.0 collective-permute-done.partner_ref
  70.8 1.4 %shard_map.40 = f32[2048,256]{1,0:T(8,128)} custom-call(f32[2048,256]{1,0:T(8,128)S(1)} %copy-done, f32[512,256]{1,0:T(8,128)S(1)} %collective-permute-done.partner_ref, bf16[512,256]{1,0:T(8,128)(2,1)S(1)} %get-tuple-element.18.high_ref, bf16[512,256]{1,0:T(8,128)(2,1)S(1)} %get-tuple-element.19.low_ref, ...), custom_call_target="tpu_custom_call", output_to_operand_aliasing={{}: (4, {})} | custom-call | flops 1610612736 | bytes 2097152 | tf_op jit(solution)/shard_map/pallas_call | solution.py:426
Async XLA Ops:
  0.7 1.6 %copy-start = (f32[2048,256]{1,0:T(8,128)S(1)}, f32[2048,256]{1,0:T(8,128)}, u32[]{:S(2)}) copy-start(f32[2048,256]{1,0:T(8,128)} %x_ref.3) | copy-start | bytes 6291460
  2.3 0.7 copy-start.1
  55.7 15.1 %collective-permute-start = (f32[512,256]{1,0:T(8,128)S(1)}, f32[512,256]{1,0:T(8,128)S(1)}, u32[]{:S(2)}, u32[]{:S(2)}) collective-permute-start(f32[512,256]{1,0:T(8,128)S(1)} %get-tuple-element.13), channel_id=1, source_target_pairs={{0,16},{16,0},{1,17},{17,1},{2,18},{18,2},{3,19},{19,3},{4,20},{20... | collective-permute-start | bytes 1572872 | tf_op jit(solution)/shard_map/ppermute | solution.py:481

commit v4 on v3

--- a/solution.py
+++ b/solution.py
@@ -196,20 +196,29 @@
         kept.append(pltpu.make_async_copy(came.at[at], near_ref.at[at], near_sem.at[c]))
         kept[-1].start()
 
-    def cross(c):
-        swaps[c].wait()
-        keep(c)
-        mine = x_ref[pl.ds(pl.multiple_of(pos * half + c * piece, piece), piece), :]
-        theirs = came[c * piece:(c + 1) * piece, :]
+    def cross(c, count=2):
+        for i in range(c, c + count):
+            swaps[i].wait()
+            keep(i)
+        mine = x_ref[pl.ds(pl.multiple_of(pos * half + c * piece, piece), count * piece), :]
+        theirs = came[c * piece:(c + count) * piece, :]
         left = jnp.where(pos == 0, mine, theirs)
         right = jnp.where(pos == 0, theirs, mine)
-        return dot3(left, right, ROWS_DIM)
-
+        return dot3(left.T, right)
+
+    mul = functools.partial(lax.dot_general, dimension_numbers=PLAIN, preferred_element_type=jnp.float32)
     own = jnp.zeros((width, width), jnp.float32)
-    for t in range(rows // piece):
-        loads[t].wait()
-        block = split(x_ref[t * piece:(t + 1) * piece, :])
-        own = own + dot_split(block, block, ROWS_DIM)
+    rest = jnp.zeros((width, width), jnp.float32)
+    tall = half // 2
+    for t in range(rows // tall):
+        for i in range(t * (tall // piece), (t + 1) * (tall // piece)):
+            loads[i].wait()
+        block = x_ref[t * tall:(t + 1) * tall, :]
+        high, low = split(block)
+        across = block.T.astype(jnp.bfloat16)
+        own = own + mul(across, high)
+        rest = rest + mul(across, low)
+    own = own + rest + rest.T
     dpart[...] = own.reshape(2, groups, share, width)
     copy = pair_up(dpart, dgot, 0)
     begin = pl.multiple_of(pos * half + EXTRA * piece, piece)
@@ -217,19 +226,19 @@
         x_ref.at[pl.ds(begin, half - EXTRA * piece)], late_ref, side_sem.at[1]
     )
     aside.start()
-    total = cross(0) + cross(1)
+    total = cross(0)
     copy.wait()
     dmid[...] = dpart[core] + dgot[...]
     copies = scatter(dmid, dnear, 0)
     total = total + cross(2)
     dfull[core, group] = summed(dmid, dnear, copies)
     copies = gather(dfull, 0)
-    total = total + cross(3) + cross(4)
+    total = total + cross(4)
     copy = hand_over(dfull, copies, 1)
     copy.wait()
     d_swap = remote(dfull, dother, one_send.at[1], one_recv.at[1], partner)
     late = [swap(c) for c in range(CHUNKS, CHUNKS + SOON)]
-    for c in range(5, CHUNKS):
+    for c in range(6, CHUNKS, 2):
         total = total + cross(c)
     cpart[...] = total.reshape(2, groups, share, width)
     copy = pair_up(cpart, cgot, 2)
@@ -251,7 +260,7 @@
             [polar(diag[:BW, BW:], left_square, right_square, left_label, meta_out[p, 0:1, BW:])]
         )
         turn_ref[p] = q
-        diag_ref[p] = dot6(q, dot6(diag, q), ROWS_DIM)
+        diag_ref[p] = dot6(q.T, dot6(diag, q))
 
     begin_round(pos)
     cmine[...] = summed(cmid, cnear, copies)
@@ -321,11 +330,46 @@
     return out
 
 
-def chain_kernel(diag_ref, cross_ref, turn_ref, meta_ref, high_ref, low_ref, g, w, lab, squares):
+def place(first, i, tile, rows):
+    blocks = rows // tile
+    at = lax.rem(lax.axis_index("blk") * (blocks // 2) + first + i, blocks)
+    return pl.ds(pl.multiple_of(at * tile, tile), tile)
+
+
+def fetch(first, count, tile, x_hbm, x_ref, sems):
+    loads = []
+    for i in range(count):
+        source = x_hbm.at[place(first, i, tile, x_hbm.shape[0])]
+        loads.append(pltpu.make_async_copy(source, x_ref.at[pl.ds(i * tile, tile)], sems.at[i]))
+        loads[-1].start()
+    return loads
+
+
+def turn_rows(
+    first, count, tile, loads, x_ref, partner_ref, high_ref, low_ref, held, out_ref, sems
+):
+    copies = []
+    for i in range(count):
+        here = slice(i * tile, i * tile + tile)
+        loads[i].wait()
+        data = split(jnp.concatenate([x_ref[here, :], partner_ref[here, :]], 1))
+        held[here, :] = dot_split(data, (high_ref[...], low_ref[...]))
+        target = out_ref.at[place(first, i, tile, out_ref.shape[0])]
+        copies.append(pltpu.make_async_copy(held.at[pl.ds(i * tile, tile)], target, sems.at[i]))
+        copies[-1].start()
+    for copy in copies:
+        copy.wait()
+
+
+def chain_kernel(
+    count, tile, diag_ref, cross_ref, turn_ref, meta_ref, x_hbm, near_ref, out_ref, high_ref, low_ref,
+    g, w, lab, squares, x_ref, held, load_sem, store_sem,
+):
     pos = lax.axis_index("blk")
+    loads = fetch(0, count, tile, x_hbm, x_ref, load_sem)
     width = 2 * BW
     small = eye(BW)
-    between = dot6(turn_ref[0], dot6(cross_ref[...], turn_ref[1]), ROWS_DIM)
+    between = dot6(turn_ref[0].T, dot6(cross_ref[...], turn_ref[1]))
     for i in range(4):
         p, s = divmod(i, 2)
         rows = slice(s * BW, s * BW + BW)
@@ -365,6 +409,7 @@
     slots = step([[0, 1], [2, 3]], 0)
     for r in range(1, ROUNDS - 1):
         qs = rotations([generator(*slots[p]) for p in range(2)])
+        backs = [q.T for q in qs]
         last = r + 2 == ROUNDS
         for p, q in ((0, 0), (1, 1), (0, 1)):
             (a, b), (c, d) = slots[p], slots[q]
@@ -377,7 +422,7 @@
                 squares[a] = jnp.broadcast_to(square[:, :BW], (8, BW))
                 squares[b] = jnp.broadcast_to(square[:, BW:], (8, BW))
                 continue
-            block = dot6(qs[p], block, ROWS_DIM)
+            block = dot6(backs[p], block)
             for i, e in enumerate((a, b)):
                 for j, f in enumerate((c, d)):
                     value = block[i * BW:(i + 1) * BW, j * BW:(j + 1) * BW]
@@ -399,45 +444,17 @@
         high, low = split(dot_split(split(jnp.concatenate([w[a, rows], w[b, rows]], 1)), cut))
         high_ref[p * width:(p + 1) * width] = high
         low_ref[p * width:(p + 1) * width] = low
-
-
-def apply_kernel(first, count, tile, x_ref, partner_ref, high_ref, low_ref, *rest):
-    out_ref, held, sems = rest[-3:]
-    rows = x_ref.shape[0]
-    blocks = rows // tile
-    pos = lax.axis_index("blk")
-    copies = []
-    for i in range(count):
-        there = pl.multiple_of(lax.rem(pos * (blocks // 2) + first + i, blocks) * tile, tile)
-        here = slice(i * tile, i * tile + tile)
-        data = split(jnp.concatenate([x_ref[pl.ds(there, tile), :], partner_ref[here, :]], 1))
-        held[here, :] = dot_split(data, (high_ref[...], low_ref[...]))
-        copies.append(
-            pltpu.make_async_copy(held.at[here], out_ref.at[pl.ds(there, tile)], sems.at[i])
-        )
-        copies[-1].start()
-    for copy in copies:
-        copy.wait()
-
-
-def apply(first, count, tile, snapshots, partner, high, low, out=None):
-    rows, width = snapshots.shape
-    extra = () if out is None else (out,)
-    return pl.pallas_call(
-        functools.partial(apply_kernel, first, count, tile),
-        out_shape=jax.ShapeDtypeStruct((rows, width), jnp.float32),
-        in_specs=[VMEM] * 4 + [ANY] * len(extra),
-        out_specs=ANY,
-        scratch_shapes=[
-            pltpu.VMEM((count * tile, width), jnp.float32), pltpu.SemaphoreType.DMA((count,)),
-        ],
-        input_output_aliases={} if out is None else {4: 0},
-        compiler_params=pltpu.CompilerParams(vmem_limit_bytes=24 * 1024 * 1024),
-        cost_estimate=pl.CostEstimate(
-            flops=count * tile * width * width * 48, bytes_accessed=count * tile * width * 16,
-            transcendentals=0,
-        ),
-    )(snapshots, partner, high, low, *extra)
+    turn_rows(0, count, tile, loads, x_ref, near_ref, high_ref, low_ref, held, out_ref, store_sem)
+
+
+def apply_kernel(
+    first, count, tile, x_hbm, partner_ref, high_ref, low_ref, into_ref, out_ref,
+    x_ref, held, load_sem, store_sem,
+):
+    loads = fetch(first, count, tile, x_hbm, x_ref, load_sem)
+    turn_rows(
+        first, count, tile, loads, x_ref, partner_ref, high_ref, low_ref, held, out_ref, store_sem
+    )
 
 
 def pair_body(n, snapshots, grades, mover):
@@ -479,25 +496,42 @@
         ),
     )(snapshots, grades.reshape(1, width), mover)
     far = lax.ppermute(late, "blk", [(0, 1), (1, 0)])
-    high, low = pl.pallas_call(
-        chain_kernel,
-        out_shape=(jax.ShapeDtypeStruct((2 * width, width), jnp.bfloat16),) * 2,
-        in_specs=[VMEM] * 4,
-        out_specs=(VMEM, VMEM),
+    done = early // tile
+    left = rows // tile - done
+    basis = jax.ShapeDtypeStruct((rows, width), f32)
+    weights = jax.ShapeDtypeStruct((2 * width, width), jnp.bfloat16)
+
+    def room(count):
+        return [
+            pltpu.VMEM((count * tile, width), f32), pltpu.VMEM((count * tile, width), f32),
+            dma((count,)), dma((count,)),
+        ]
+
+    out, high, low = pl.pallas_call(
+        functools.partial(chain_kernel, done, tile),
+        out_shape=(basis, weights, weights),
+        in_specs=[VMEM] * 4 + [HBM, VMEM],
+        out_specs=(HBM, VMEM, VMEM),
         scratch_shapes=[
             pltpu.VMEM((16, BW, BW), f32),
             pltpu.VMEM((4, 2 * width, BW), f32),
             pltpu.VMEM((4, BW, BW), f32),
             pltpu.VMEM((4, 8, BW), f32),
-        ],
-        compiler_params=pltpu.CompilerParams(vmem_limit_bytes=32 * 1024 * 1024),
+        ] + room(done),
+        compiler_params=pltpu.CompilerParams(vmem_limit_bytes=36 * 1024 * 1024),
         cost_estimate=pl.CostEstimate(
-            flops=15 * 10**9, bytes_accessed=4 * width * width * 8, transcendentals=0
+            flops=18 * 10**9, bytes_accessed=4 * width * width * 8, transcendentals=0
         ),
-    )(diag, cross, turn, meta)
-    done = early // tile
-    out = apply(0, done, tile, snapshots, near, high, low)
-    return apply(done, rows // tile - done, tile, snapshots, far, high, low, out)
+    )(diag, cross, turn, meta, snapshots, near)
+    return pl.pallas_call(
+        functools.partial(apply_kernel, done, left, tile),
+        out_shape=basis,
+        in_specs=[HBM, VMEM, VMEM, VMEM, HBM],
+        out_specs=HBM,
+        scratch_shapes=room(left),
+        input_output_aliases={4: 0},
+        compiler_params=pltpu.CompilerParams(vmem_limit_bytes=24 * 1024 * 1024),
+    )(snapshots, far, high, low, out)
 
 
 def solution(mesh):

time: 72.6 us -> 74.9 us (1.032)
  Pallas kernels: 68.3 us -> 70.8 us
    pallas_call x3 -> x2, Pallas kernels: 15.7 us -> 18.3 us  [the longest x1 16.4 us: pair_body(): pl.pallas_call(functools.partial(chain_kernel, done, tile), out_shape=(ba...]
    unnamed x5 -> x7, local copies, waits for them, and re-layouts: 3.01 us -> 3.01 us
  transfers between devices with their start and end apart: 1 -> 1, of which waited for: 0 -> 0; matrix products, arithmetic and copies ran while one was open for 0% -> 0% of each run, Pallas kernels for 20% -> 22%
where the time goes in v4:
time: 74.9 us; the launch traced here: 74.7 us
  Pallas kernels  70.8 us (95%)
  local copies, waits for them, and re-layouts  3.01 us (4%)
  starting transfers between devices  0.75 us (1%)
    pallas_call x1, Pallas kernels, pair_body(): pl.pallas_call(functools.partial(gram_kernel, n), out_shape=(squares, squ...  52.5 us
    pallas_call x1, Pallas kernels, pair_body(): pl.pallas_call(functools.partial(chain_kernel, done, tile), out_shape=(ba...  16.4 us
    unnamed x7, local copies, waits for them, and re-layouts  3.01 us
    pallas_call x1, Pallas kernels, pair_body(): pl.pallas_call(functools.partial(apply_kernel, done, left, tile), out_sha...  1.91 us
  transfers between devices with their start and end apart: 1, of which 0 were waited for; matrix products, arithmetic and copies ran while one was open for 0% of the time, Pallas kernels for 22%

profile of v4, /device:TPU:0, one launch (start us, length us, event | category | flops | bytes accessed | tf_op | source)
XLA Modules:
  0.0 74.7 jit_solution(14113087190907637825)
XLA Ops:
  0.0 0.7 copy.5.mover_ref
  0.7 0.0 copy-start
  0.7 1.6 %copy-done = f32[2048,256]{1,0:T(8,128)S(1)} copy-done((f32[2048,256]{1,0:T(8,128)S(1)}, f32[2048,256]{1,0:T(8,128)}, u32[]{:S(2)}) %copy-start) | copy-done | bytes 2097176
  2.3 0.0 copy-start.2
  2.3 0.7 copy-done.2
  3.0 0.0 copy-start.1
  3.0 52.5 %shard_map.37 = (f32[2,256,256]{2,1,0:T(8,128)S(1)}, f32[256,256]{1,0:T(8,128)S(1)}, f32[2,256,256]{2,1,0:T(8,128)S(1)}, f32[2,8,256]{2,1,0:T(8,128)S(1)}, f32[1...) custom-call(f32[2048,256]{1,0:T(8,128)S(1)} %copy-done, s32[1,256]{1,0:T(1,128)S(1)} %bitcast.1, s32[3,1]{1,0:T(4,128)S(1)} %copy.5.mover_ref), custom_call_target="tpu_custom_call" | custom-call | tf_op jit(solution)/shard_map/pallas_call | solution.py:474
  55.5 0.8 %collective-permute-start = (f32[512,256]{1,0:T(8,128)S(1)}, f32[512,256]{1,0:T(8,128)S(1)}, u32[]{:S(2)}, u32[]{:S(2)}) collective-permute-start(f32[512,256]{1,0:T(8,128)S(1)} %get-tuple-element.14), channel_id=1, source_target_pairs={{0,16},{16,0},{1,17},{17,1},{2,18},{18,2},{3,19},{19,3},{4,20},{20... | collective-permute-start | bytes 1572872 | tf_op jit(solution)/shard_map/ppermute | solution.py:498
  56.2 0.0 copy-done.1
  56.2 16.4 %shard_map.38 = (f32[2048,256]{1,0:T(8,128)}, bf16[512,256]{1,0:T(8,128)(2,1)S(1)}, bf16[512,256]{1,0:T(8,128)(2,1)S(1)}) custom-call(f32[2,256,256]{2,1,0:T(8,128)S(1)} %get-tuple-element.15.diag_ref, f32[256,256]{1,0:T(8,128)S(1)} %get-tuple-element.16.cross_ref, f32[2,256,256]{2,1,0:T(8,128)S(1)} %get-tuple-element.17.turn_ref, ...), custom_call_target="tpu_custom_call" | custom-call | flops 17999998976 | bytes 2097152 | tf_op jit(solution)/shard_map/pallas_call | solution.py:510
  72.7 0.0 collective-permute-done.partner_ref
  72.7 1.9 %shard_map.39 = f32[2048,256]{1,0:T(8,128)} custom-call(f32[2048,256]{1,0:T(8,128)S(1)} %copy-done.1, f32[512,256]{1,0:T(8,128)S(1)} %collective-permute-done.partner_ref, bf16[512,256]{1,0:T(8,128)(2,1)S(1)} %get-tuple-element.20.high_ref, bf16[512,256]{1,0:T(8,128)(2,1)S(1)} %get-tuple-element.21.low_ref, ...), custom_call_target="tpu_custom_call", output_to_operand_aliasing={{}: (4, {})} | custom-call | tf_op jit(solution)/shard_map/pallas_call | solution.py:526
Async XLA Ops:
  0.7 1.6 %copy-start = (f32[2048,256]{1,0:T(8,128)S(1)}, f32[2048,256]{1,0:T(8,128)}, u32[]{:S(2)}) copy-start(f32[2048,256]{1,0:T(8,128)} %x_hbm.5) | copy-start | bytes 6291460
  2.3 0.7 copy-start.2
  3.0 53.2 %copy-start.1 = (f32[2048,256]{1,0:T(8,128)S(1)}, f32[2048,256]{1,0:T(8,128)}, u32[]{:S(2)}) copy-start(f32[2048,256]{1,0:T(8,128)} %x_hbm.5) | copy-start | bytes 6291460
  55.5 17.2 %collective-permute-start = (f32[512,256]{1,0:T(8,128)S(1)}, f32[512,256]{1,0:T(8,128)S(1)}, u32[]{:S(2)}, u32[]{:S(2)}) collective-permute-start(f32[512,256]{1,0:T(8,128)S(1)} %get-tuple-element.14), channel_id=1, source_target_pairs={{0,16},{16,0},{1,17},{17,1},{2,18},{18,2},{3,19},{19,3},{4,20},{20... | collective-permute-start | bytes 1572872 | tf_op jit(solution)/shard_map/ppermute | solution.py:498

commit v5 on v3

--- a/solution.py
+++ b/solution.py
@@ -103,11 +103,11 @@
 
 
 def gram_kernel(
-    n, x_hbm, grade_ref, mover_ref, diag_ref, cross_ref, turn_ref, meta_out, near_ref, late_ref,
-    x_ref, grade, came, meta, meta_got, dpart, dgot, dmid, dnear, dfull, dother,
+    n, x_ref, grade_ref, mover_ref, diag_ref, cross_ref, turn_ref, meta_out, near_ref, late_ref,
+    meta, meta_got, dpart, dgot, dmid, dnear, dfull, dother,
     cpart, cgot, cmid, cnear, cmine, cother, cfull,
     x_send, x_recv, rs_send, rs_recv, ag_send, ag_recv, sib_send, sib_recv, one_send, one_recv,
-    load_sem, near_sem, side_sem,
+    side_sem,
 ):
     pos, me = lax.axis_index("blk"), lax.axis_index("rows")
     other = 1 - pos
@@ -120,22 +120,13 @@
     partner, sibling = (other, me), (pos, me + 1 - 2 * core)
     peers = [None] + [lax.rem(group + k, groups) for k in range(1, groups)]
 
-    grade_load = pltpu.make_async_copy(grade_ref, grade, side_sem.at[0])
-    grade_load.start()
-    loads = []
-    for t in range(rows // piece):
-        at = pl.ds(t * piece, piece)
-        loads.append(pltpu.make_async_copy(x_hbm.at[at], x_ref.at[at], load_sem.at[t]))
-        loads[-1].start()
-
     barrier = pltpu.get_barrier_semaphore()
     for peer in peers[1:]:
         pl.semaphore_signal(barrier, inc=1, device_id=(pos, 2 * peer + core), device_id_type=MESH)
     for device in (partner, sibling):
         pl.semaphore_signal(barrier, inc=1, device_id=device, device_id_type=MESH)
     meta[...] = jnp.zeros_like(meta)
-    grade_load.wait()
-    meta[0:1, :] = grade[...].astype(jnp.float32)
+    meta[0:1, :] = grade_ref[...].astype(jnp.float32)
     for r in range(ROUNDS - 1):
         meta[r + 1:r + 2, :] = jnp.full((1, width), mover_ref[r, 0], jnp.int32).astype(jnp.float32)
     pl.semaphore_wait(barrier, groups + 1)
@@ -150,8 +141,8 @@
 
     def swap(c):
         start = lax.rem(other * half + c * piece, rows)
-        source = x_hbm.at[pl.ds(pl.multiple_of(start, piece), piece)]
-        return remote(source, came.at[pl.ds(c * piece, piece)], x_send.at[c], x_recv.at[c], partner)
+        source = x_ref.at[pl.ds(pl.multiple_of(start, piece), piece)]
+        return remote(source, near_ref.at[pl.ds(c * piece, piece)], x_send.at[c], x_recv.at[c], partner)
 
     labels = remote(meta, meta_got, one_send.at[0], one_recv.at[0], partner)
     swaps = [swap(c) for c in range(CHUNKS)]
@@ -189,34 +180,20 @@
             copy.wait()
         return remote(full.at[core], full.at[core], sib_send.at[which], sib_recv.at[which], sibling)
 
-    kept = []
-
-    def keep(c):
-        at = pl.ds(c * piece, piece)
-        kept.append(pltpu.make_async_copy(came.at[at], near_ref.at[at], near_sem.at[c]))
-        kept[-1].start()
-
     def cross(c):
         swaps[c].wait()
-        keep(c)
         mine = x_ref[pl.ds(pl.multiple_of(pos * half + c * piece, piece), piece), :]
-        theirs = came[c * piece:(c + 1) * piece, :]
+        theirs = near_ref[c * piece:(c + 1) * piece, :]
         left = jnp.where(pos == 0, mine, theirs)
         right = jnp.where(pos == 0, theirs, mine)
         return dot3(left, right, ROWS_DIM)
 
     own = jnp.zeros((width, width), jnp.float32)
     for t in range(rows // piece):
-        loads[t].wait()
         block = split(x_ref[t * piece:(t + 1) * piece, :])
         own = own + dot_split(block, block, ROWS_DIM)
     dpart[...] = own.reshape(2, groups, share, width)
     copy = pair_up(dpart, dgot, 0)
-    begin = pl.multiple_of(pos * half + EXTRA * piece, piece)
-    aside = pltpu.make_async_copy(
-        x_ref.at[pl.ds(begin, half - EXTRA * piece)], late_ref, side_sem.at[1]
-    )
-    aside.start()
     total = cross(0) + cross(1)
     copy.wait()
     dmid[...] = dpart[core] + dgot[...]
@@ -240,6 +217,11 @@
     copy.wait()
     cmid[...] = cpart[core] + cgot[...]
     copies = scatter(cmid, cnear, 1)
+    begin = pl.multiple_of(pos * half + EXTRA * piece, piece)
+    aside = pltpu.make_async_copy(
+        x_ref.at[pl.ds(begin, half - EXTRA * piece)], late_ref, side_sem.at[1]
+    )
+    aside.start()
     unit = eye(BW)
 
     def begin_round(p):
@@ -266,12 +248,9 @@
     copy = hand_over(cfull, copies, 3)
     for c in range(EXTRA):
         late[c].wait()
-        keep(CHUNKS + c)
     copy.wait()
     cross_ref[...] = cfull[...].reshape(width, width)
     aside.wait()
-    for copy in kept:
-        copy.wait()
 
 
 def polar(cross_gram, left_square, right_square, left_label, right_label):
@@ -462,17 +441,16 @@
             jax.ShapeDtypeStruct((early, width), f32),
             jax.ShapeDtypeStruct((rows - early, width), f32),
         ),
-        in_specs=[HBM, HBM, pl.BlockSpec(memory_space=pltpu.SMEM)],
-        out_specs=(VMEM, VMEM, VMEM, VMEM, ANY, ANY),
+        in_specs=[VMEM, VMEM, pl.BlockSpec(memory_space=pltpu.SMEM)],
+        out_specs=(VMEM, VMEM, VMEM, VMEM, VMEM, ANY),
         scratch_shapes=[
-            pltpu.VMEM((rows, width), f32), pltpu.VMEM((1, width), jnp.int32),
-            pltpu.VMEM((early, width), f32), pltpu.VMEM((8, width), f32), pltpu.VMEM((8, width), f32),
+            pltpu.VMEM((8, width), f32), pltpu.VMEM((8, width), f32),
             whole, part, part, part, whole, whole,
             whole, part, part, part, one, one, whole,
             dma((CHUNKS + EXTRA,)), dma((CHUNKS + EXTRA,)),
             dma((2, n // 2)), dma((2, n // 2)), dma((2, n // 2)), dma((2, n // 2)),
             dma((4,)), dma((4,)), dma((3,)), dma((3,)),
-            dma((2 * CHUNKS,)), dma((CHUNKS + EXTRA,)), dma((2,)),
+            dma((2,)),
         ],
         compiler_params=pltpu.CompilerParams(
             collective_id=0, has_side_effects=True, vmem_limit_bytes=40 * 1024 * 1024

time: 72.6 us -> 69.1 us (0.952)
  Pallas kernels: 68.3 us -> 65 us
    pallas_call x1, Pallas kernels: 52.6 us -> 49.3 us  [pair_body(): pl.pallas_call(functools.partial(gram_kernel, n), out_shape=(squares, squ...]
  transfers between devices with their start and end apart: 1 -> 1, of which waited for: 0 -> 0; matrix products, arithmetic and copies ran while one was open for 0% -> 0% of each run, Pallas kernels for 20% -> 21%
where the time goes in v5:
time: 69.1 us; the launch traced here: 68.9 us
  Pallas kernels  65 us (94%)
  local copies, waits for them, and re-layouts  3.01 us (4%)
    pallas_call x1, Pallas kernels, pair_body(): pl.pallas_call(functools.partial(gram_kernel, n), out_shape=(squares, squ...  49.3 us
    pallas_call x1, Pallas kernels, pair_body(): pl.pallas_call(chain_kernel, out_shape=(jax.ShapeDtypeStruct((2 * width,...  12 us
    pallas_call x2, Pallas kernels, apply(): pl.pallas_call(functools.partial(apply_kernel, first, count, tile), out_s...  3.73 us
    unnamed x5, local copies, waits for them, and re-layouts  3.01 us
  transfers between devices with their start and end apart: 1, of which 0 were waited for; matrix products, arithmetic and copies ran while one was open for 0% of the time, Pallas kernels for 21%

profile of v5, /device:TPU:0, one launch (start us, length us, event | category | flops | bytes accessed | tf_op | source)
XLA Modules:
  0.0 68.9 jit_solution(15629925004358427266)
XLA Ops:
  0.0 0.7 %copy.5.mover_ref = s32[3,1]{1,0:T(4,128)S(1)} copy(s32[3,1]{0,1:T(1,128)} %param.5) | data formatting | bytes 24 | tf_op args[2]
  0.7 0.0 copy-start
  0.7 1.6 %copy-done = f32[2048,256]{1,0:T(8,128)S(1)} copy-done((f32[2048,256]{1,0:T(8,128)S(1)}, f32[2048,256]{1,0:T(8,128)}, u32[]{:S(2)}) %copy-start) | copy-done | bytes 2097176
  2.3 0.0 copy-start.1
  2.3 0.7 copy-done.1
  3.0 49.3 %shard_map.37 = (f32[2,256,256]{2,1,0:T(8,128)S(1)}, f32[256,256]{1,0:T(8,128)S(1)}, f32[2,256,256]{2,1,0:T(8,128)S(1)}, f32[2,8,256]{2,1,0:T(8,128)S(1)}, f32[1...) custom-call(f32[2048,256]{1,0:T(8,128)S(1)} %copy-done, s32[1,256]{1,0:T(1,128)S(1)} %bitcast.1, s32[3,1]{1,0:T(4,128)S(1)} %copy.5.mover_ref), custom_call_target="tpu_custom_call" | custom-call | tf_op jit(solution)/shard_map/pallas_call | solution.py:436
  52.4 0.7 collective-permute-start
  53.0 12.0 %shard_map.38 = (bf16[512,256]{1,0:T(8,128)(2,1)S(1)}, bf16[512,256]{1,0:T(8,128)(2,1)S(1)}) custom-call(f32[2,256,256]{2,1,0:T(8,128)S(1)} %get-tuple-element.14.diag_ref, f32[256,256]{1,0:T(8,128)S(1)} %get-tuple-element.15.cross_ref, f32[2,256,256]{2,1,0:T(8,128)S(1)} %get-tuple-element.16.turn_ref, f32[2,8,256]{2,1,0:T(8,128)S(1)} %get-tuple-element.17.meta_ref), custom_call_target="tpu_custom_call" | custom-call | flops 15000000512 | bytes 2097152 | tf_op jit(solution)/shard_map/pallas_call | solution.py:460
  65.0 2.3 %shard_map.39.rest_0_ = f32[2048,256]{1,0:T(8,128)} custom-call(f32[2048,256]{1,0:T(8,128)S(1)} %copy-done, f32[1536,256]{1,0:T(8,128)S(1)} %get-tuple-element.20.partner_ref, bf16[512,256]{1,0:T(8,128)(2,1)S(1)} %get-tuple-element.18.high_ref, bf16[512,256]{1,0:T(8,128)(2,1)S(1)} %get-tuple-element.19.low_ref), custom_call_target="tpu_custom_call" | custom-call | flops 4831838208 | bytes 6291456 | tf_op jit(solution)/shard_map/pallas_call | solution.py:405
  67.3 0.0 collective-permute-done.partner_ref
  67.3 1.4 %shard_map.40 = f32[2048,256]{1,0:T(8,128)} custom-call(f32[2048,256]{1,0:T(8,128)S(1)} %copy-done, f32[512,256]{1,0:T(8,128)S(1)} %collective-permute-done.partner_ref, bf16[512,256]{1,0:T(8,128)(2,1)S(1)} %get-tuple-element.18.high_ref, bf16[512,256]{1,0:T(8,128)(2,1)S(1)} %get-tuple-element.19.low_ref, ...), custom_call_target="tpu_custom_call", output_to_operand_aliasing={{}: (4, {})} | custom-call | flops 1610612736 | bytes 2097152 | tf_op jit(solution)/shard_map/pallas_call | solution.py:405
Async XLA Ops:
  0.7 1.6 %copy-start = (f32[2048,256]{1,0:T(8,128)S(1)}, f32[2048,256]{1,0:T(8,128)}, u32[]{:S(2)}) copy-start(f32[2048,256]{1,0:T(8,128)} %x_ref.5) | copy-start | bytes 6291460
  2.3 0.7 copy-start.1
  52.4 15.0 %collective-permute-start = (f32[512,256]{1,0:T(8,128)S(1)}, f32[512,256]{1,0:T(8,128)S(1)}, u32[]{:S(2)}, u32[]{:S(2)}) collective-permute-start(f32[512,256]{1,0:T(8,128)S(1)} %get-tuple-element.13), channel_id=1, source_target_pairs={{0,16},{16,0},{1,17},{17,1},{2,18},{18,2},{3,19},{19,3},{4,20},{20... | collective-permute-start | bytes 1572872 | tf_op jit(solution)/shard_map/ppermute | solution.py:459
